TPU v7x, 32 devices: a whole 2x2x4 slice. The times are simulated.
32 devices in a mesh: ctx: 8 (over z, y), fsdp: 4 (over x, core).
Axes of the slice: x: 2, y: 2, z: 4, core: 2. Of those that a mesh axis runs over, the one named last changes fastest.
Arguments:
- tokens: bfloat16 [4, 1024, 2048], P('fsdp', 'ctx'), may hold values from -6 to 6
- cotangent: bfloat16 [4, 1024, 2048], P('fsdp', 'ctx'), may hold values from -6 to 6
- pair_table: int32 [8], replicated, may hold values from 0 to 7, each once
- doc_lengths: int32 [4, 3], P('fsdp'), may hold values from 1 to 512, 1024 in all within a row
- attn_gain: bfloat16 [2048], P('fsdp'), may hold values from 0.099609375 to 1.8984375
- query_weight: bfloat16 [2048, 2048], P('fsdp'), may hold values from -0.125 to 0.125
- key_matrix: bfloat16 [2048, 512], P('fsdp'), may hold values from -0.125 to 0.125
- value_matrix: bfloat16 [2048, 512], P('fsdp'), may hold values from -0.125 to 0.125
- output_weight: bfloat16 [2048, 2048], P('fsdp'), may hold values from -1 to 1
- mlp_gain: bfloat16 [2048], P('fsdp'), may hold values from 0.099609375 to 1.8984375
- gate_weight: bfloat16 [2048, 8192], P('fsdp'), may hold values from -0.125 to 0.125
- up_weight: bfloat16 [2048, 8192], P('fsdp'), may hold values from -0.125 to 0.125
- down_weight: bfloat16 [8192, 2048], P('fsdp'), may hold values from -0.0625 to 0.0625
Outputs:
- output: bfloat16 [4, 1024, 2048], P('fsdp', 'ctx')
- input_grad: bfloat16 [4, 1024, 2048], P('fsdp', 'ctx')
- attn_gain_grad: float32 [2048], P(('ctx', 'fsdp'))
- query_weight_grad: float32 [2048, 2048], P(('ctx', 'fsdp'))
- key_weight_grad: float32 [2048, 512], P(('ctx', 'fsdp'))
- value_weight_grad: float32 [2048, 512], P(('ctx', 'fsdp'))
- output_weight_grad: float32 [2048, 2048], P(('ctx', 'fsdp'))
- mlp_gain_grad: float32 [2048], P(('ctx', 'fsdp'))
- gate_weight_grad: float32 [2048, 8192], P(('ctx', 'fsdp'))
- up_weight_grad: float32 [2048, 8192], P(('ctx', 'fsdp'))
- down_weight_grad: float32 [8192, 2048], P(('ctx', 'fsdp'))
Inputs may be any that keep to these rules, and one draw needn't show every extreme that they name: `pair_table`: each index of ctx appears exactly once. `doc_lengths`: the 3 documents of a sequence fill its 1024 positions in order; in every sequence one document has exactly 512 positions.
All inputs are finite; a program needn't handle non-finite values.
Results may differ from a plain program's by a relative error of at most 0.017.
Values may be sent and summed in bfloat16 or wider, within the bound.
No kernel may reach another device: no remote copies, remote signals or barrier semaphores. Data moves between devices by JAX's collectives and lax.ppermute only.
A program may use at most 512 MiB of HBM per device.

v0:
```python
import math

import jax
import jax.numpy as jnp
from jax import lax
from jax.sharding import PartitionSpec as P

MODEL_WIDTH = 2048
QUERY_HEADS = 32
KEY_VALUE_HEADS = 8
HEAD_SIZE = 64


epsilon = 1e-05
masked_score = -1e30


def rms_forward(values_in, norm_gain):
    scale_row = lax.rsqrt(jnp.mean(values_in * values_in, axis=-1, keepdims=True) + epsilon)
    return (values_in * scale_row * norm_gain, scale_row)


def rms_backward(values_in, scale_row, norm_gain, grad_normed):
    weighted = grad_normed * norm_gain
    inner_sum = jnp.mean(weighted * values_in, axis=-1, keepdims=True)
    grad_values = scale_row * weighted - values_in * scale_row * scale_row * scale_row * inner_sum
    grad_gain = jnp.sum(grad_normed * values_in * scale_row, axis=0)
    return (grad_values, grad_gain)


def rope_tables(rot_places, half_dim):
    frequency = 1.0 / 500000.0 ** (jnp.arange(half_dim, dtype=jnp.float32) * 2.0 / (2 * half_dim))
    angles = rot_places.astype(jnp.float32)[..., None] * frequency
    return (jnp.cos(angles), jnp.sin(angles))


def apply_rotation(vectors, cosine_table, sine_table):
    half_dim = vectors.shape[-1] // 2
    front_half = vectors[..., :half_dim]
    back_half = vectors[..., half_dim:]
    cos_heads = cosine_table[..., None, :]
    sin_heads = sine_table[..., None, :]
    return jnp.concatenate(
        [
            front_half * cos_heads - back_half * sin_heads,
            back_half * cos_heads + front_half * sin_heads,
        ],
        axis=-1,
    )


def inverse_rotation(vectors, cosine_table, sine_table):
    half_dim = vectors.shape[-1] // 2
    front_half = vectors[..., :half_dim]
    back_half = vectors[..., half_dim:]
    cos_heads = cosine_table[..., None, :]
    sin_heads = sine_table[..., None, :]
    return jnp.concatenate(
        [
            front_half * cos_heads + back_half * sin_heads,
            back_half * cos_heads - front_half * sin_heads,
        ],
        axis=-1,
    )


def layout_places(pair_table, block_len, sequence_length):
    row_ids = jnp.arange(sequence_length, dtype=jnp.int32)
    shard_ids = row_ids // (2 * block_len)
    within = row_ids % (2 * block_len)
    num_devices = pair_table.shape[0]
    device_ids = jnp.arange(num_devices, dtype=jnp.int32)
    chosen = jnp.sum(
        jnp.where(shard_ids[:, None] == device_ids[None, :], pair_table[None, :], 0), axis=1
    )
    block_ids = jnp.where(within < block_len, chosen, 2 * num_devices - 1 - chosen)
    return block_ids * block_len + within % block_len


def document_places(places, lengths_row):
    doc_ends = jnp.cumsum(lengths_row)
    doc_starts = doc_ends - lengths_row
    doc_ids = jnp.sum((places[:, None] >= doc_ends[None, :]).astype(jnp.int32), axis=1)
    doc_numbers = jnp.arange(lengths_row.shape[0], dtype=jnp.int32)
    picked = jnp.sum(
        jnp.where(doc_ids[:, None] == doc_numbers[None, :], doc_starts[None, :], 0), axis=1
    )
    return (doc_ids, places - picked)


def to_items(head_leading_layout, sequence_count, shard_length, query_group_width):
    reshaped_tensor = head_leading_layout.reshape(
        sequence_count, shard_length, KEY_VALUE_HEADS, query_group_width, HEAD_SIZE
    )
    return reshaped_tensor.transpose(0, 2, 3, 1, 4).reshape(
        sequence_count * KEY_VALUE_HEADS, query_group_width * shard_length, HEAD_SIZE
    )


def from_items(element_rows, sequence_count, shard_length, query_group_width):
    reshaped_tensor = element_rows.reshape(
        sequence_count, KEY_VALUE_HEADS, query_group_width, shard_length, HEAD_SIZE
    )
    return reshaped_tensor.transpose(0, 3, 1, 2, 4).reshape(
        sequence_count, shard_length, QUERY_HEADS, HEAD_SIZE
    )


def body(
    tokens,
    cotangent,
    pair_table,
    doc_lengths,
    attn_gain,
    query_weight,
    key_matrix,
    value_matrix,
    output_weight,
    mlp_gain,
    gate_weight,
    up_weight,
    down_weight,
):
    sequence_count = tokens.shape[0]
    shard_length = tokens.shape[1]
    block_len = shard_length // 2
    ctx_count = lax.axis_size("ctx")
    sequence_length = shard_length * ctx_count
    query_group_width = QUERY_HEADS // KEY_VALUE_HEADS
    token_total = sequence_count * shard_length
    score_scale = 1.0 / math.sqrt(HEAD_SIZE)
    ctx_start = lax.axis_index("ctx") * shard_length
    places = layout_places(pair_table, block_len, sequence_length)
    key_document_ids, key_rot = jax.vmap(document_places, in_axes=(None, 0))(places, doc_lengths)
    query_places = lax.dynamic_slice_in_dim(places, ctx_start, shard_length)
    query_document_ids = lax.dynamic_slice_in_dim(key_document_ids, ctx_start, shard_length, axis=1)
    query_rot = lax.dynamic_slice_in_dim(key_rot, ctx_start, shard_length, axis=1)
    cosine_table, sine_table = rope_tables(query_rot, HEAD_SIZE // 2)
    row_places = jnp.tile(query_places, query_group_width)
    row_document_ids = jnp.repeat(
        jnp.tile(query_document_ids, (1, query_group_width)), KEY_VALUE_HEADS, axis=0
    )
    column_document_ids = jnp.repeat(key_document_ids, KEY_VALUE_HEADS, axis=0)
    full_weights = (
        lax.all_gather(attn_gain, "fsdp", axis=0, tiled=True),
        lax.all_gather(query_weight, "fsdp", axis=0, tiled=True),
        lax.all_gather(key_matrix, "fsdp", axis=0, tiled=True),
        lax.all_gather(value_matrix, "fsdp", axis=0, tiled=True),
        lax.all_gather(output_weight, "fsdp", axis=0, tiled=True),
        lax.all_gather(mlp_gain, "fsdp", axis=0, tiled=True),
        lax.all_gather(gate_weight, "fsdp", axis=0, tiled=True),
        lax.all_gather(up_weight, "fsdp", axis=0, tiled=True),
        lax.all_gather(down_weight, "fsdp", axis=0, tiled=True),
    )
    (
        attn_full,
        query_full,
        key_full,
        value_full,
        output_full,
        mlp_full,
        gate_full,
        up_full,
        down_full,
    ) = full_weights
    attn_gain_f = attn_full.astype(jnp.float32)
    mlp_gain_f = mlp_full.astype(jnp.float32)

    def weight_term(left_rows, right_rows):
        return jnp.einsum("tr,tc->rc", left_rows, right_rows, preferred_element_type=jnp.float32)

    inputs = tokens.reshape(token_total, MODEL_WIDTH).astype(jnp.float32)
    first_normalized, scale_one = rms_forward(inputs, attn_gain_f)
    first_normalized = first_normalized.astype(jnp.bfloat16)
    queries = jnp.dot(first_normalized, query_full, preferred_element_type=jnp.float32)
    key_unrotated = jnp.dot(first_normalized, key_full, preferred_element_type=jnp.float32)
    value_unprojected = jnp.dot(first_normalized, value_full, preferred_element_type=jnp.float32)
    query_rotated_rows = apply_rotation(
        queries.reshape(sequence_count, shard_length, QUERY_HEADS, HEAD_SIZE),
        cosine_table,
        sine_table,
    ).astype(jnp.bfloat16)
    key_rotated_rows = apply_rotation(
        key_unrotated.reshape(sequence_count, shard_length, KEY_VALUE_HEADS, HEAD_SIZE),
        cosine_table,
        sine_table,
    ).astype(jnp.bfloat16)
    value_reduced = value_unprojected.astype(jnp.bfloat16).reshape(
        sequence_count, shard_length, KEY_VALUE_HEADS, HEAD_SIZE
    )
    key_outgoing = key_rotated_rows.transpose(0, 2, 1, 3).reshape(
        sequence_count, KEY_VALUE_HEADS, shard_length * HEAD_SIZE
    )
    value_outgoing = value_reduced.transpose(0, 2, 1, 3).reshape(
        sequence_count, KEY_VALUE_HEADS, shard_length * HEAD_SIZE
    )
    key_gathered, value_gathered = (
        lax.all_gather(key_outgoing, "ctx", axis=2, tiled=True),
        lax.all_gather(value_outgoing, "ctx", axis=2, tiled=True),
    )
    key_elements = key_gathered.reshape(
        sequence_count * KEY_VALUE_HEADS, sequence_length, HEAD_SIZE
    )
    value_elements = value_gathered.reshape(
        sequence_count * KEY_VALUE_HEADS, sequence_length, HEAD_SIZE
    )
    query_items = to_items(query_rotated_rows, sequence_count, shard_length, query_group_width)

    def scores_of(query_rows, key_rows, row_doc, col_doc):
        raw_scores = (
            jnp.einsum("rd,ld->rl", query_rows, key_rows, preferred_element_type=jnp.float32)
            * score_scale
        )
        allowed = (places[None, :] <= row_places[:, None]) & (col_doc[None, :] == row_doc[:, None])
        return jnp.where(allowed, raw_scores, masked_score)

    def attend(operands):
        query_rows, key_rows, value_rows, row_doc, col_doc = operands
        scores = scores_of(query_rows, key_rows, row_doc, col_doc)
        row_max = jnp.max(scores, axis=1, keepdims=True)
        exponent = jnp.exp(scores - row_max)
        row_total = jnp.sum(exponent, axis=1, keepdims=True)
        attn_weights = (exponent / row_total).astype(jnp.bfloat16)
        mixed_rows = jnp.einsum(
            "rl,ld->rd", attn_weights, value_rows, preferred_element_type=jnp.float32
        )
        return (mixed_rows, (row_max + jnp.log(row_total))[:, 0])

    mixed_items, log_totals = lax.map(
        attend, (query_items, key_elements, value_elements, row_document_ids, column_document_ids)
    )
    attn_mixed = (
        from_items(mixed_items, sequence_count, shard_length, query_group_width)
        .reshape(token_total, QUERY_HEADS * HEAD_SIZE)
        .astype(jnp.bfloat16)
    )
    hidden = inputs + jnp.dot(attn_mixed, output_full, preferred_element_type=jnp.float32)
    normed_two, scale_two = rms_forward(hidden, mlp_gain_f)
    normed_two = normed_two.astype(jnp.bfloat16)
    grad_out = cotangent.reshape(token_total, MODEL_WIDTH)
    gate_proj = jnp.dot(normed_two, gate_full, preferred_element_type=jnp.float32)
    up_proj = jnp.dot(normed_two, up_full, preferred_element_type=jnp.float32)
    activated = (jax.nn.silu(gate_proj) * up_proj).astype(jnp.bfloat16)
    branch_term = jnp.dot(activated, down_full, preferred_element_type=jnp.float32)
    output = (hidden + branch_term).astype(jnp.bfloat16)
    grad_act = jnp.einsum("tc,fc->tf", grad_out, down_full, preferred_element_type=jnp.float32)
    sigmoid_gate = jax.nn.sigmoid(gate_proj)
    grad_up = (grad_act * (gate_proj * sigmoid_gate)).astype(jnp.bfloat16)
    grad_gate = (
        grad_act * up_proj * sigmoid_gate * (1.0 + gate_proj * (1.0 - sigmoid_gate))
    ).astype(jnp.bfloat16)
    normed_term = jnp.einsum(
        "tf,df->td", grad_gate, gate_full, preferred_element_type=jnp.float32
    ) + jnp.einsum("tf,df->td", grad_up, up_full, preferred_element_type=jnp.float32)
    grad_hidden_part, mlp_gain_grad = rms_backward(hidden, scale_two, mlp_gain_f, normed_term)
    gate_piece = weight_term(normed_two, grad_gate)
    up_piece = weight_term(normed_two, grad_up)
    mlp_gain_out, gate_out, up_out = (
        lax.psum_scatter(mlp_gain_grad, ("ctx", "fsdp"), scatter_dimension=0, tiled=True),
        lax.psum_scatter(gate_piece, ("ctx", "fsdp"), scatter_dimension=0, tiled=True),
        lax.psum_scatter(up_piece, ("ctx", "fsdp"), scatter_dimension=0, tiled=True),
    )
    down_out = None
    grad_hidden = grad_out.astype(jnp.float32) + grad_hidden_part
    grad_branch = grad_hidden.astype(jnp.bfloat16)
    grad_mixed = jnp.einsum(
        "tc,hc->th", grad_branch, output_full, preferred_element_type=jnp.float32
    ).astype(jnp.bfloat16)
    grad_items = to_items(
        grad_mixed.reshape(sequence_count, shard_length, QUERY_HEADS, HEAD_SIZE),
        sequence_count,
        shard_length,
        query_group_width,
    )

    def attend_back(operands):
        query_rows, key_rows, value_rows, row_doc, col_doc, grad_rows, log_total = operands
        scores = scores_of(query_rows, key_rows, row_doc, col_doc)
        attn_probs = jnp.exp(scores - log_total[:, None])
        grad_probs = jnp.einsum(
            "rd,ld->rl", grad_rows, value_rows, preferred_element_type=jnp.float32
        )
        inner_sum = jnp.sum(attn_probs * grad_probs, axis=1, keepdims=True)
        grad_scores = (attn_probs * (grad_probs - inner_sum)).astype(jnp.bfloat16)
        grad_query = (
            jnp.einsum("rl,ld->rd", grad_scores, key_rows, preferred_element_type=jnp.float32)
            * score_scale
        )
        grad_key = (
            jnp.einsum("rl,rd->ld", grad_scores, query_rows, preferred_element_type=jnp.float32)
            * score_scale
        )
        grad_value = jnp.einsum(
            "rl,rd->ld",
            attn_probs.astype(jnp.bfloat16),
            grad_rows,
            preferred_element_type=jnp.float32,
        )
        return (grad_query, grad_key, grad_value)

    query_term, key_contribution, value_contribution = lax.map(
        attend_back,
        (
            query_items,
            key_elements,
            value_elements,
            row_document_ids,
            column_document_ids,
            grad_items,
            log_totals,
        ),
    )
    key_contribution = key_contribution.reshape(
        sequence_count, KEY_VALUE_HEADS, sequence_length * HEAD_SIZE
    )
    value_contribution = value_contribution.reshape(
        sequence_count, KEY_VALUE_HEADS, sequence_length * HEAD_SIZE
    )
    key_gradient_total, value_gradient_total = (
        lax.psum_scatter(
            key_contribution.astype(jnp.bfloat16), "ctx", scatter_dimension=2, tiled=True
        ).astype(jnp.float32),
        lax.psum_scatter(
            value_contribution.astype(jnp.bfloat16), "ctx", scatter_dimension=2, tiled=True
        ).astype(jnp.float32),
    )
    key_gradient_total = key_gradient_total.reshape(
        sequence_count, KEY_VALUE_HEADS, shard_length, HEAD_SIZE
    ).transpose(0, 2, 1, 3)
    key_grad = (
        inverse_rotation(key_gradient_total, cosine_table, sine_table)
        .astype(jnp.bfloat16)
        .reshape(token_total, KEY_VALUE_HEADS * HEAD_SIZE)
    )
    value_grad = (
        value_gradient_total.reshape(sequence_count, KEY_VALUE_HEADS, shard_length, HEAD_SIZE)
        .transpose(0, 2, 1, 3)
        .astype(jnp.bfloat16)
        .reshape(token_total, KEY_VALUE_HEADS * HEAD_SIZE)
    )
    query_grad = inverse_rotation(
        from_items(query_term, sequence_count, shard_length, query_group_width),
        cosine_table,
        sine_table,
    )
    query_grad = query_grad.astype(jnp.bfloat16).reshape(token_total, QUERY_HEADS * HEAD_SIZE)
    grad_normed_one = (
        jnp.einsum("th,dh->td", query_grad, query_full, preferred_element_type=jnp.float32)
        + jnp.einsum("th,dh->td", key_grad, key_full, preferred_element_type=jnp.float32)
        + jnp.einsum("th,dh->td", value_grad, value_full, preferred_element_type=jnp.float32)
    )
    grad_input_part, attn_gain_grad = rms_backward(inputs, scale_one, attn_gain_f, grad_normed_one)
    input_grad = (grad_hidden + grad_input_part).astype(jnp.bfloat16).reshape(tokens.shape)
    tail_term = weight_term(activated, grad_out)
    query_piece = weight_term(first_normalized, query_grad)
    key_piece = weight_term(first_normalized, key_grad)
    value_piece = weight_term(first_normalized, value_grad)
    output_piece = weight_term(attn_mixed, grad_branch)
    attn_shards = (
        lax.psum_scatter(attn_gain_grad, ("ctx", "fsdp"), scatter_dimension=0, tiled=True),
        lax.psum_scatter(query_piece, ("ctx", "fsdp"), scatter_dimension=0, tiled=True),
        lax.psum_scatter(key_piece, ("ctx", "fsdp"), scatter_dimension=0, tiled=True),
        lax.psum_scatter(value_piece, ("ctx", "fsdp"), scatter_dimension=0, tiled=True),
        lax.psum_scatter(output_piece, ("ctx", "fsdp"), scatter_dimension=0, tiled=True),
        lax.psum_scatter(tail_term, ("ctx", "fsdp"), scatter_dimension=0, tiled=True),
    )
    down_out = attn_shards[5]
    output = output.reshape(tokens.shape)
    return (
        output,
        input_grad,
        attn_shards[0],
        attn_shards[1],
        attn_shards[2],
        attn_shards[3],
        attn_shards[4],
        mlp_gain_out,
        gate_out,
        up_out,
        down_out,
    )


def solution(mesh):
    return jax.shard_map(
        body,
        mesh=mesh,
        in_specs=(
            P("fsdp", "ctx", None),
            P("fsdp", "ctx", None),
            P(),
            P("fsdp", None),
            P("fsdp"),
            P("fsdp", None),
            P("fsdp", None),
            P("fsdp", None),
            P("fsdp", None),
            P("fsdp"),
            P("fsdp", None),
            P("fsdp", None),
            P("fsdp", None),
        ),
        out_specs=(
            P("fsdp", "ctx", None),
            P("fsdp", "ctx", None),
            P(("ctx", "fsdp")),
            P(("ctx", "fsdp"), None),
            P(("ctx", "fsdp"), None),
            P(("ctx", "fsdp"), None),
            P(("ctx", "fsdp"), None),
            P(("ctx", "fsdp")),
            P(("ctx", "fsdp"), None),
            P(("ctx", "fsdp"), None),
            P(("ctx", "fsdp"), None),
        ),
        check_vma=False,
    )
```

profile of v0, /device:TPU:14, one launch (start us, length us, event | category | flops | bytes accessed | tf_op | source)
XLA Modules:
  0.0 3944.2 jit_solution(9870470707789165231)
XLA Ops:
  10.2 5.2 all-gather
  18.5 13.8 all-gather.14.cloned.1.call-done
  32.3 3.0 copy.73
  37.4 19.1 all-gather.18.cloned.1.call-done
  56.5 2.1 convolution_convert_fusion.1
  63.5 5.2 all-gather.1
  69.5 28.8 all-gather.16.cloned.1.call-done
  98.3 3.2 reshape.730
  101.5 38.4 all-gather.20.cloned.1.call-done
  139.9 4.5 reshape.733
  144.4 55.1 %all-gather.12.cloned.1.call-done = bf16[2048,2048]{1,0:T(8,128)(2,1)} async-done(((bf16[512,2048]{1,0:T(8,128)(2,1)}), bf16[2048,2048]{1,0:T(8,128)(2,1)}) %all-gather.12.cloned.1.call-update) | async-done | bytes 8388624 | tf_op jit(solution)/shard_map/all_gather | solution.py:146
  199.5 12.4 copy.71
  211.9 7.1 convolution_bitcast_fusion.2
  220.6 35.8 while.30
  222.7 2.2 fusion.176
  227.2 2.2 fusion.176
  231.6 2.2 fusion.176
  236.1 2.2 fusion.176
  240.5 2.2 fusion.176
  245.0 2.2 fusion.176
  249.4 2.2 fusion.176
  253.8 2.2 fusion.176
  259.2 4.7 multiply_reduce_fusion.3
  264.1 198.2 %all-gather.24.cloned.1.call-done = bf16[2048,8192]{1,0:T(8,128)(2,1)} async-done(((bf16[512,8192]{1,0:T(8,128)(2,1)}), bf16[2048,8192]{1,0:T(8,128)(2,1)}) %all-gather.24.cloned.1.call-update) | async-done | bytes 33554448 | tf_op jit(solution)/shard_map/all_gather | solution.py:151
  462.3 18.7 fusion.101
  481.0 184.4 %all-gather.26.cloned.1.call-done = bf16[2048,8192]{1,0:T(8,128)(2,1)} async-done(((bf16[512,8192]{1,0:T(8,128)(2,1)}), bf16[2048,8192]{1,0:T(8,128)(2,1)}) %all-gather.26.cloned.1.call-update) | async-done | bytes 33554448 | tf_op jit(solution)/shard_map/all_gather | solution.py:152
  665.4 18.7 fusion.102
  684.1 184.4 %all-gather.28.cloned.1.call-done = bf16[8192,2048]{1,0:T(8,128)(2,1)} async-done(((bf16[2048,2048]{1,0:T(8,128)(2,1)}), bf16[8192,2048]{1,0:T(8,128)(2,1)}) %all-gather.28.cloned.1.call-update) | async-done | bytes 33554448 | tf_op jit(solution)/shard_map/all_gather | solution.py:153
  868.5 21.3 multiply_convert_fusion.1
  889.8 16.3 fusion.103
  906.1 17.3 multiply_reduce_fusion.1
  923.7 6.3 convolution_convert_fusion
  932.5 69.9 %while.31 = (s32[]{:T(128)}, f32[8,512,64]{1,2,0:T(8,128)}, bf16[8,1024,64]{1,2,0:T(8,128)(2,1)}, bf16[8,1024,64]{1,2,0:T(8,128)(2,1)}, s32[1024]{0:T(1024)S(1)}...) while((s32[]{:T(128)}, f32[8,512,64]{1,2,0:T(8,128)}, ...), condition=%wide.region_13.14_spmd.clone.clone, body=%wide.region_11.13_spmd.clone.sunk.clone | while | flops 341933568 | bytes 17737360 | solution.py:301
  934.2 2.0 multiply_reduce_fusion.6
  936.5 2.1 fusion.186
  945.2 2.1 fusion.186
  953.9 2.1 fusion.186
  962.6 2.1 fusion.186
  971.3 2.1 fusion.186
  977.7 2.0 multiply_reduce_fusion.6
  980.0 2.1 fusion.186
  988.7 2.1 fusion.186
  997.4 2.1 fusion.186
  1002.4 2.7 copy.82
  1005.1 4.2 convert_element_type.219
  1011.2 4.2 convert_element_type.223
  1015.4 59.0 %reduce-scatter.10.cloned.1.call-done = bf16[1,8,8192]{2,1,0:T(8,128)(2,1)} async-done(((bf16[1,8,65536]{2,1,0:T(8,128)(2,1)}), bf16[1,8,8192]{2,1,0:T(8,128)(2,1)}) %reduce-scatter.10.cloned.1.call-update) | async-done | bytes 131088 | tf_op jit(solution)/shard_map/reduce_scatter | solution.py:320
  1075.8 2.8 fusion.73
  1078.6 62.4 %reduce-scatter.12.cloned.1.call-done = bf16[1,8,8192]{2,1,0:T(8,128)(2,1)} async-done(((bf16[1,8,65536]{2,1,0:T(8,128)(2,1)}), bf16[1,8,8192]{2,1,0:T(8,128)(2,1)}) %reduce-scatter.12.cloned.1.call-update) | async-done | bytes 131088 | tf_op jit(solution)/shard_map/reduce_scatter | solution.py:323
  1142.4 2.7 fusion.71
  1149.2 8.2 fusion.69
  1158.4 8.0 fusion.77
  1166.6 25.0 fusion.105
  1191.7 25.0 fusion.106
  1217.7 25.0 fusion.63
  1242.7 6.5 fusion.104
  1249.3 14.1 fusion.42
  1266.0 39.4 all-reduce.2
  1307.8 86.8 %reduce-scatter.18.cloned.1.call-done = f32[64,512]{1,0:T(8,128)} async-done(((f32[2048,512]{1,0:T(8,128)}), f32[64,512]{1,0:T(8,128)}) %reduce-scatter.18.cloned.1.call-update) | async-done | bytes 131088 | tf_op jit(solution)/shard_map/reduce_scatter | solution.py:363
  1394.6 216.3 %reduce-scatter.14.cloned.1.call-done = f32[64,2048]{1,0:T(8,128)} async-done(((f32[2048,2048]{1,0:T(8,128)}), f32[64,2048]{1,0:T(8,128)}) %reduce-scatter.14.cloned.1.call-update) | async-done | bytes 524304 | tf_op jit(solution)/shard_map/reduce_scatter | solution.py:361
  1610.9 187.4 %reduce-scatter.20.cloned.1.call-done = f32[64,2048]{1,0:T(8,128)} async-done(((f32[2048,2048]{1,0:T(8,128)}), f32[64,2048]{1,0:T(8,128)}) %reduce-scatter.20.cloned.1.call-update) | async-done | bytes 524304 | tf_op jit(solution)/shard_map/reduce_scatter | solution.py:364
  1798.2 712.3 %reduce-scatter.22.cloned.1.call-done = f32[64,8192]{1,0:T(8,128)} async-done(((f32[2048,8192]{1,0:T(8,128)}), f32[64,8192]{1,0:T(8,128)}) %reduce-scatter.22.cloned.1.call-update) | async-done | bytes 2097168 | tf_op jit(solution)/shard_map/reduce_scatter | solution.py:260
  2510.5 713.2 %reduce-scatter.24.cloned.1.call-done = f32[64,8192]{1,0:T(8,128)} async-done(((f32[2048,8192]{1,0:T(8,128)}), f32[64,8192]{1,0:T(8,128)}) %reduce-scatter.24.cloned.1.call-update) | async-done | bytes 2097168 | tf_op jit(solution)/shard_map/reduce_scatter | solution.py:261
  3223.7 713.2 %reduce-scatter.26.cloned.1.call-done = f32[256,2048]{1,0:T(8,128)} async-done(((f32[8192,2048]{1,0:T(8,128)}), f32[256,2048]{1,0:T(8,128)}) %reduce-scatter.26.cloned.1.call-update) | async-done | bytes 2097168 | tf_op jit(solution)/shard_map/reduce_scatter | solution.py:365
  (269 shorter events, 103.1 us)
Async XLA Ops:
  7.2 25.2 all-gather.14.cloned.1.call-start
  7.9 48.6 %all-gather.18.cloned.1.call-start = ((), (), s32[]{:S(2)}) async-start(), calls=%async_computation.12 | async-start | bytes 2621440 | tf_op jit(solution)/shard_map/all_gather | solution.py:148
  8.7 89.7 %all-gather.16.cloned.1.call-start = ((), (), s32[]{:S(2)}) async-start(), calls=%async_computation.11 | async-start | bytes 1179648 | tf_op jit(solution)/shard_map/all_gather | solution.py:198
  32.3 3.0 copy-start
  37.4 102.6 %all-gather.20.cloned.1.call-start = ((), (), s32[]{:S(2)}) async-start(), calls=%async_computation.13 | async-start | bytes 1179648 | tf_op jit(solution)/shard_map/all_gather | solution.py:199
  59.8 139.6 %all-gather.12.cloned.1.call-start = ((), (), s32[]{:S(2)}) async-start(), calls=%async_computation.9 | async-start | bytes 10485760 | tf_op jit(solution)/shard_map/all_gather | solution.py:146
  60.4 198.8 %all-gather.22.cloned.1.call-start = ((), (), s32[]{:S(2)}) async-start(), calls=%async_computation.14 | async-start | bytes 10485760 | tf_op jit(solution)/shard_map/all_gather | solution.py:149
  61.0 401.3 %all-gather.24.cloned.1.call-start = ((), (), s32[]{:S(2)}) async-start(), calls=%async_computation.15 | async-start | bytes 41943040 | tf_op jit(solution)/shard_map/all_gather | solution.py:151
  61.8 603.6 %all-gather.26.cloned.1.call-start = ((), (), s32[]{:S(2)}) async-start(), calls=%async_computation.16 | async-start | bytes 41943040 | tf_op jit(solution)/shard_map/all_gather | solution.py:152
  62.5 1.0 copy-start.19
  62.5 806.0 %all-gather.28.cloned.1.call-start = ((), (), s32[]{:S(2)}) async-start(), calls=%async_computation.17 | async-start | bytes 41943040 | tf_op jit(solution)/shard_map/all_gather | solution.py:153
  63.2 1011.1 %reduce-scatter.10.cloned.1.call-start = ((), (), s32[]{:S(2)}) async-start(), calls=%async_computation.18 | async-start | bytes 1179648 | tf_op jit(solution)/shard_map/reduce_scatter | solution.py:320
  256.3 1.6 copy-start.7
  258.0 5.9 copy-start.5
  263.9 659.4 %copy-start.1 = (f32[128,2048]{1,0:T(8,128)}, f32[128,2048]{1,0:T(8,128)S(1)}, u32[]{:S(2)}) copy-start(f32[128,2048]{1,0:T(8,128)S(1)} %get-tuple-element.299) | copy-start | bytes 3145732
  481.0 387.5 %copy-start.8 = (bf16[1,128,2048]{2,1,0:T(8,128)(2,1)S(1)}, bf16[1,128,2048]{2,1,0:T(8,128)(2,1)}, u32[]{:S(2)}) copy-start(bf16[1,128,2048]{2,1,0:T(8,128)(2,1)} %param.18) | copy-start | bytes 1572868
  906.1 17.3 copy-start.9
  1005.1 4.3 copy-start.16
  1009.3 131.7 %reduce-scatter.12.cloned.1.call-start = ((), (), s32[]{:S(2)}) async-start(), calls=%async_computation.19 | async-start | bytes 1179648 | tf_op jit(solution)/shard_map/reduce_scatter | solution.py:323
  1015.4 292.4 %reduce-scatter.16.cloned.1.call-start = ((), (), s32[]{:S(2)}) async-start(), calls=%async_computation.21 | async-start | bytes 4325376 | tf_op jit(solution)/shard_map/reduce_scatter | solution.py:362
  1075.8 2.8 copy-start.14
  1078.6 316.0 %reduce-scatter.18.cloned.1.call-start = ((), (), s32[]{:S(2)}) async-start(), calls=%async_computation.22 | async-start | bytes 4325376 | tf_op jit(solution)/shard_map/reduce_scatter | solution.py:363
  1142.4 2.7 copy-start.12
  1145.1 1.2 copy-start.17
  1145.1 465.8 %reduce-scatter.14.cloned.1.call-start = ((), (), s32[]{:S(2)}) async-start(), calls=%async_computation.20 | async-start | bytes 17301504 | tf_op jit(solution)/shard_map/reduce_scatter | solution.py:361
  1157.4 1.0 copy-start.6
  1157.4 640.8 %reduce-scatter.20.cloned.1.call-start = ((), (), s32[]{:S(2)}) async-start(), calls=%async_computation.23 | async-start | bytes 17301504 | tf_op jit(solution)/shard_map/reduce_scatter | solution.py:364
  1166.5 1344.0 %reduce-scatter.22.cloned.1.call-start = ((), (), s32[]{:S(2)}) async-start(), calls=%async_computation.24 | async-start | bytes 69206016 | tf_op jit(solution)/shard_map/reduce_scatter | solution.py:260
  1191.6 2032.1 %reduce-scatter.24.cloned.1.call-start = ((), (), s32[]{:S(2)}) async-start(), calls=%async_computation.25 | async-start | bytes 69206016 | tf_op jit(solution)/shard_map/reduce_scatter | solution.py:261
  1216.7 1.0 copy-start.10
  1216.7 2720.3 %reduce-scatter.26.cloned.1.call-start = ((), (), s32[]{:S(2)}) async-start(), calls=%async_computation.26 | async-start | bytes 69206016 | tf_op jit(solution)/shard_map/reduce_scatter | solution.py:365
  1242.7 6.5 copy-start.2
  1242.7 6.5 copy-start.3
  1249.2 14.1 copy-start.4
  1249.3 14.1 copy-start.15
  1263.4 1.6 copy-start.11
  1263.4 1.6 copy-start.13
  1265.0 1.0 copy-start.18
Sparse Core Ops, SparseCore 0:
  9.5 22.7 all-gather.13
  33.9 22.5 all-gather.17
  59.2 39.1 all-gather.15
  100.9 38.9 all-gather.19
  141.3 58.1 all-gather.11
  200.9 58.2 all-gather.21
  260.7 201.4 all-gather.23
  463.8 201.4 all-gather.25
  666.9 201.4 all-gather.27
  1009.5 64.8 reduce-scatter.9
  1077.8 63.1 reduce-scatter.11
  1143.7 108.8 reduce-scatter.15
  1255.5 139.0 reduce-scatter.17
  1397.3 213.5 reduce-scatter.13
  1613.6 184.5 reduce-scatter.19
  1801.0 709.4 reduce-scatter.21
  2513.3 710.3 reduce-scatter.23
  3226.5 710.3 reduce-scatter.25
where the time goes:
time: 3960 us; the launch traced here: 3940 us
  waiting for transfers between devices  3480 us (88%)
  matrix products  330 us (8%)
  local copies, waits for them, and re-layouts  55.2 us (1%)
  blocking collectives  49.8 us (1%)
    reduce_scatter x1, waiting for transfers between devices, body(): lax.psum_scatter(tail_term, ('ctx', 'fsdp'), scatter_dimension=0, tiled=T...  713 us
    reduce_scatter x1, waiting for transfers between devices, body(): lax.psum_scatter(up_piece, ('ctx', 'fsdp'), scatter_dimension=0, tiled=True)  713 us
    reduce_scatter x1, waiting for transfers between devices, body(): lax.psum_scatter(gate_piece, ('ctx', 'fsdp'), scatter_dimension=0, tiled=...  712 us
    reduce_scatter x1, waiting for transfers between devices, body(): lax.psum_scatter(query_piece, ('ctx', 'fsdp'), scatter_dimension=0, tiled...  216 us
    all_gather x1, waiting for transfers between devices, body(): lax.all_gather(gate_weight, 'fsdp', axis=0, tiled=True)  198 us
    reduce_scatter x1, waiting for transfers between devices, body(): lax.psum_scatter(output_piece, ('ctx', 'fsdp'), scatter_dimension=0, tile...  187 us
    all_gather x1, waiting for transfers between devices, body(): lax.all_gather(down_weight, 'fsdp', axis=0, tiled=True)  184 us
    all_gather x1, waiting for transfers between devices, body(): lax.all_gather(up_weight, 'fsdp', axis=0, tiled=True)  184 us
  transfers between devices with their start and end apart: 18, of which 17 were waited for; matrix products, arithmetic and copies ran while one was open for 6% of the time, Pallas kernels for 0%

commit v1 on v0

v1 whole, which is shorter than its diff:
```python
import math

import jax
import jax.numpy as jnp
from jax import lax
from jax.sharding import Mesh
from jax.sharding import PartitionSpec as P

MODEL_WIDTH = 2048
QUERY_HEADS = 32
KEY_VALUE_HEADS = 8
HEAD_SIZE = 64


epsilon = 1e-05
masked_score = -1e30


def rms_forward(values_in, norm_gain):
    scale_row = lax.rsqrt(jnp.mean(values_in * values_in, axis=-1, keepdims=True) + epsilon)
    return (values_in * scale_row * norm_gain, scale_row)


def rms_backward(values_in, scale_row, norm_gain, grad_normed):
    weighted = grad_normed * norm_gain
    inner_sum = jnp.mean(weighted * values_in, axis=-1, keepdims=True)
    grad_values = scale_row * weighted - values_in * scale_row * scale_row * scale_row * inner_sum
    grad_gain = jnp.sum(grad_normed * values_in * scale_row, axis=0)
    return (grad_values, grad_gain)


def rope_tables(rot_places, half_dim):
    frequency = 1.0 / 500000.0 ** (jnp.arange(half_dim, dtype=jnp.float32) * 2.0 / (2 * half_dim))
    angles = rot_places.astype(jnp.float32)[..., None] * frequency
    return (jnp.cos(angles), jnp.sin(angles))


def apply_rotation(vectors, cosine_table, sine_table):
    half_dim = vectors.shape[-1] // 2
    front_half = vectors[..., :half_dim]
    back_half = vectors[..., half_dim:]
    cos_heads = cosine_table[..., None, :]
    sin_heads = sine_table[..., None, :]
    return jnp.concatenate(
        [
            front_half * cos_heads - back_half * sin_heads,
            back_half * cos_heads + front_half * sin_heads,
        ],
        axis=-1,
    )


def inverse_rotation(vectors, cosine_table, sine_table):
    half_dim = vectors.shape[-1] // 2
    front_half = vectors[..., :half_dim]
    back_half = vectors[..., half_dim:]
    cos_heads = cosine_table[..., None, :]
    sin_heads = sine_table[..., None, :]
    return jnp.concatenate(
        [
            front_half * cos_heads + back_half * sin_heads,
            back_half * cos_heads - front_half * sin_heads,
        ],
        axis=-1,
    )


def layout_places(pair_table, block_len, sequence_length):
    row_ids = jnp.arange(sequence_length, dtype=jnp.int32)
    shard_ids = row_ids // (2 * block_len)
    within = row_ids % (2 * block_len)
    num_devices = pair_table.shape[0]
    device_ids = jnp.arange(num_devices, dtype=jnp.int32)
    chosen = jnp.sum(
        jnp.where(shard_ids[:, None] == device_ids[None, :], pair_table[None, :], 0), axis=1
    )
    block_ids = jnp.where(within < block_len, chosen, 2 * num_devices - 1 - chosen)
    return block_ids * block_len + within % block_len


def document_places(places, lengths_row):
    doc_ends = jnp.cumsum(lengths_row)
    doc_starts = doc_ends - lengths_row
    doc_ids = jnp.sum((places[:, None] >= doc_ends[None, :]).astype(jnp.int32), axis=1)
    doc_numbers = jnp.arange(lengths_row.shape[0], dtype=jnp.int32)
    picked = jnp.sum(
        jnp.where(doc_ids[:, None] == doc_numbers[None, :], doc_starts[None, :], 0), axis=1
    )
    return (doc_ids, places - picked)


EVERY = ("c", "x", "k")
CHIPS = ("c", "x")


class Wires:
    def __init__(self, ctx_count):
        self.count = ctx_count
        self.total = ctx_count * 4
        self.paths = ctx_count == 8
        self.c = lax.axis_index("c")
        self.x = lax.axis_index("x")
        self.k = lax.axis_index("k")
        self.f = 2 * self.x + self.k
        if self.paths:
            z_of = lambda i: i >> 3
            middle = [i for i in range(32) if z_of(i) in (1, 2)]
            ends = [i for i in range(32) if z_of(i) in (0, 3)]
            self.mid = [(i, i ^ 24) for i in middle]
            self.outward = [(i, i ^ 8) for i in middle]
            self.inward = [(i, i ^ 8) for i in ends]
            z_index = self.c // 2
            self.inner = (z_index == 1) | (z_index == 2)

    def swap(self, value, bits):
        return lax.ppermute(value, EVERY, [(i, i ^ bits) for i in range(self.total)])

    def send(self, value, pairs):
        return lax.ppermute(value, EVERY, pairs)

    def over_fsdp(self, shard):
        other = self.swap(shard, 2)
        near = self.x == 0
        both = jnp.stack([jnp.where(near, shard, other), jnp.where(near, other, shard)])
        partner = self.swap(both, 1)
        first = self.k == 0
        even = jnp.where(first, both, partner)
        odd = jnp.where(first, partner, both)
        return jnp.stack([even, odd], axis=1).reshape((-1,) + shard.shape[1:])

    def sum_fsdp(self, parts, axis):
        grid = jnp.moveaxis(parts, axis, 0)
        grid = grid.reshape((2, 2) + grid.shape[1:])
        mine = lax.dynamic_index_in_dim(grid, self.k, 1, keepdims=False)
        theirs = lax.dynamic_index_in_dim(grid, 1 - self.k, 1, keepdims=False)
        pair_sum = mine + self.swap(theirs, 1)
        mine = lax.dynamic_index_in_dim(pair_sum, self.x, 0, keepdims=False)
        theirs = lax.dynamic_index_in_dim(pair_sum, 1 - self.x, 0, keepdims=False)
        return mine + self.swap(theirs, 2)

    def ctx_gather(self, value):
        return lax.all_gather(value, "c", axis=0, tiled=False)

    def z_spread(self, value):
        step = self.swap(value, 8)
        over = self.send(value, self.mid)
        over_step = self.send(step, self.mid)
        out = self.send(over, self.outward)
        out_step = self.send(over_step, self.outward)
        second = jnp.where(self.inner, over_step, out)
        third = jnp.where(self.inner, over, out_step)
        return jnp.stack([value, step, second, third])

    def z_collect(self, parts):
        own, near, far, across = parts[0], parts[1], parts[2], parts[3]
        low = jnp.bfloat16
        wide = jnp.float32
        got = self.send(jnp.stack([far, across]).astype(low), self.inward).astype(wide)
        across = across + got[0]
        far = far + got[1]
        got = self.send(jnp.stack([across, far]).astype(low), self.mid).astype(wide)
        own = own + got[0]
        near = near + got[1]
        return own + self.swap(near.astype(low), 8).astype(wide)

    def spread(self, value):
        if not self.paths:
            return [lax.all_gather(value, CHIPS, axis=0, tiled=True)]
        half = value.shape[0] // 2
        width = value.shape[1]
        found = []
        for rows, order in ((value[:half], (4, 2)), (value[half:], (2, 4))):
            held = self.z_spread(rows)
            for bits in order:
                held = jnp.stack([held, self.swap(held, bits)])
            found.append(held.reshape(16 * half, width))
        return found

    def collect(self, parts):
        if not self.paths:
            low = parts[0].astype(jnp.bfloat16)
            return lax.psum_scatter(low, CHIPS, scatter_dimension=0, tiled=True).astype(jnp.float32)
        found = []
        for part, order in zip(parts, ((2, 4), (4, 2))):
            half = part.shape[0] // 16
            held = part.reshape(2, 2, 4, half, part.shape[1])
            for bits in order:
                held = held[0] + self.swap(held[1].astype(jnp.bfloat16), bits).astype(jnp.float32)
            found.append(self.z_collect(held))
        return jnp.concatenate(found, axis=0)


def body(
    tokens,
    cotangent,
    pair_table,
    doc_lengths,
    attn_gain,
    query_weight,
    key_matrix,
    value_matrix,
    output_weight,
    mlp_gain,
    gate_weight,
    up_weight,
    down_weight,
):
    low = jnp.bfloat16
    wide = jnp.float32
    ctx_count = lax.axis_size("c")
    wires = Wires(ctx_count)
    shard_length = tokens.shape[1]
    block_len = shard_length // 2
    length = shard_length * ctx_count
    c, x, k = wires.c, wires.x, wires.k
    heads = QUERY_HEADS // ctx_count
    head_width = heads * HEAD_SIZE
    share = max(1, ctx_count // KEY_VALUE_HEADS)
    kv_index = c // share
    kv_part = HEAD_SIZE // share
    hidden_total = gate_weight.shape[1]
    hidden_chip = hidden_total // (2 * ctx_count)
    score_scale = 1.0 / math.sqrt(HEAD_SIZE)

    def mm(left, right):
        return jnp.dot(left, right, preferred_element_type=wide)

    def mm_t(left, right):
        return jnp.einsum("ij,kj->ik", left, right, preferred_element_type=wide)

    def t_mm(left, right):
        return jnp.einsum("ti,tj->ij", left, right, preferred_element_type=wide)

    places = layout_places(pair_table, block_len, length)
    docs, rot = document_places(places, doc_lengths[0])
    cosine_table, sine_table = rope_tables(rot, HEAD_SIZE // 2)

    own = tokens[0]
    own_wide = own.astype(wide)
    dy = cotangent[0]

    rows = wires.ctx_gather(own).reshape(length, MODEL_WIDTH)
    gains = wires.over_fsdp(jnp.stack([attn_gain, mlp_gain], axis=1)).astype(wide)
    attn_gain_f = gains[:, 0]
    mlp_gain_f = gains[:, 1]
    take = lambda array, start, size: lax.dynamic_slice_in_dim(array, start, size, axis=1)
    head_weights = wires.over_fsdp(
        jnp.concatenate(
            [
                take(query_weight, c * head_width, head_width),
                take(key_matrix, kv_index * HEAD_SIZE, HEAD_SIZE),
                take(value_matrix, kv_index * HEAD_SIZE, HEAD_SIZE),
            ],
            axis=1,
        )
    )
    output_full = wires.over_fsdp(output_weight)

    normed_one, _ = rms_forward(rows.astype(wide), attn_gain_f)
    normed_one = normed_one.astype(low)
    projected = mm(normed_one, head_weights)
    q_rot = apply_rotation(
        projected[:, :head_width].reshape(length, heads, HEAD_SIZE), cosine_table, sine_table
    ).astype(low)
    k_rot = apply_rotation(
        projected[:, None, head_width : head_width + HEAD_SIZE], cosine_table, sine_table
    ).astype(low)[:, 0]
    v_low = projected[:, head_width + HEAD_SIZE :].astype(low)
    allowed = (places[None, :] <= places[:, None]) & (docs[None, :] == docs[:, None])

    def scores_of(queries):
        raw = jnp.einsum("rhd,ld->hrl", queries, k_rot, preferred_element_type=wide) * score_scale
        return jnp.where(allowed[None], raw, masked_score)

    scores = scores_of(q_rot)
    row_max = jnp.max(scores, axis=2, keepdims=True)
    exponent = jnp.exp(scores - row_max)
    row_total = jnp.sum(exponent, axis=2, keepdims=True)
    probs = exponent / row_total
    probs_low = probs.astype(low)
    mixed = (
        jnp.einsum("hrl,ld->rhd", probs_low, v_low, preferred_element_type=wide)
        .astype(low)
        .reshape(length, head_width)
    )
    mixed_rows = lax.all_to_all(mixed, "c", 0, 1, tiled=True)
    hidden = own_wide + mm(mixed_rows, output_full)
    normed_two, scale_two = rms_forward(hidden, mlp_gain_f)
    normed_two = normed_two.astype(low)

    def chip_columns(weight):
        start = hidden_chip * 2 * c
        mine = take(weight, start + hidden_chip * x, hidden_chip)
        theirs = take(weight, start + hidden_chip * (1 - x), hidden_chip)
        other = wires.swap(theirs, 2)
        near = x == 0
        both = jnp.stack([jnp.where(near, mine, other), jnp.where(near, other, mine)])
        partner = wires.swap(both, 1)
        first = k == 0
        even = jnp.where(first, both, partner)
        odd = jnp.where(first, partner, both)
        return jnp.stack([even, odd], axis=1).reshape(MODEL_WIDTH, hidden_chip)

    gate_chip = chip_columns(gate_weight)
    up_chip = chip_columns(up_weight)
    down_shard = down_weight.shape[0]
    holder = (2 * hidden_chip * c) // down_shard
    inside = 2 * hidden_chip * c - holder * down_shard
    down_mine = lax.dynamic_slice_in_dim(down_weight, inside + hidden_chip * x, hidden_chip)
    down_theirs = lax.dynamic_slice_in_dim(down_weight, inside + hidden_chip * (1 - x), hidden_chip)
    crossing = []
    for place in range(ctx_count):
        source = (2 * hidden_chip * place) // down_shard
        crossing.append((place * 4 + source, place * 4 + (source ^ 2)))
    down_other = wires.send(down_theirs, crossing)
    down_held = jnp.where(holder // 2 == x, down_mine, down_other)
    down_chip = jnp.where(holder % 2 == k, down_held, wires.swap(down_held, 1))

    normed_all = wires.spread(normed_two)
    dy_all = wires.spread(dy)
    out_parts = []
    grad_parts = []
    gate_term = 0.0
    up_term = 0.0
    down_term = 0.0
    for normed_rows, dy_rows in zip(normed_all, dy_all):
        gate_proj = mm(normed_rows, gate_chip)
        up_proj = mm(normed_rows, up_chip)
        sigmoid_gate = jax.nn.sigmoid(gate_proj)
        silu_gate = gate_proj * sigmoid_gate
        activated = (silu_gate * up_proj).astype(low)
        grad_act = mm_t(dy_rows, down_chip)
        grad_up = (grad_act * silu_gate).astype(low)
        grad_gate = (
            grad_act * up_proj * sigmoid_gate * (1.0 + gate_proj * (1.0 - sigmoid_gate))
        ).astype(low)
        out_parts.append(mm(activated, down_chip))
        grad_parts.append(mm_t(grad_gate, gate_chip) + mm_t(grad_up, up_chip))
        gate_term = gate_term + t_mm(normed_rows, grad_gate)
        up_term = up_term + t_mm(normed_rows, grad_up)
        down_term = down_term + t_mm(activated, dy_rows)
    normed_term = wires.collect(grad_parts)
    branch = wires.collect(out_parts)
    output = (hidden + branch).astype(low).reshape(tokens.shape)

    def core_sum(parts, axis):
        mine = lax.dynamic_index_in_dim(parts, k, axis, keepdims=False)
        theirs = lax.dynamic_index_in_dim(parts, 1 - k, axis, keepdims=False)
        return mine + wires.swap(theirs, 1)

    down_out = core_sum(down_term.reshape(2, hidden_chip // 2, MODEL_WIDTH), 0)
    row_count = MODEL_WIDTH // (4 * ctx_count)

    def columns_out(term):
        parts = core_sum(term.reshape(2 * ctx_count, 2, row_count, hidden_chip), 1)
        moved = lax.all_to_all(parts.astype(low), CHIPS, 0, 0, tiled=True)
        return moved.transpose(1, 0, 2).reshape(row_count, hidden_total).astype(wide)

    gate_out = columns_out(gate_term)
    up_out = columns_out(up_term)

    grad_hidden_part, mlp_gain_grad = rms_backward(hidden, scale_two, mlp_gain_f, normed_term)
    grad_hidden = dy.astype(wide) + grad_hidden_part
    grad_branch = grad_hidden.astype(low)
    grad_mixed_rows = mm_t(grad_branch, output_full).astype(low)
    grad_mixed = lax.all_to_all(grad_mixed_rows, "c", 1, 0, tiled=True)
    branch_rows = wires.ctx_gather(grad_branch).reshape(length, MODEL_WIDTH)
    output_term = t_mm(mixed, branch_rows)
    output_out = wires.sum_fsdp(output_term.reshape(4, row_count, MODEL_WIDTH), 0)

    grad_heads = grad_mixed.reshape(length, heads, HEAD_SIZE)
    grad_probs = jnp.einsum("rhd,ld->hrl", grad_heads, v_low, preferred_element_type=wide)
    inner_sum = jnp.sum(probs * grad_probs, axis=2, keepdims=True)
    grad_scores = (probs * (grad_probs - inner_sum)).astype(low)
    grad_q_rot = (
        jnp.einsum("hrl,ld->rhd", grad_scores, k_rot, preferred_element_type=wide) * score_scale
    )
    grad_k_rot = (
        jnp.einsum("hrl,rhd->ld", grad_scores, q_rot, preferred_element_type=wide) * score_scale
    )
    grad_v = jnp.einsum("hrl,rhd->ld", probs_low, grad_heads, preferred_element_type=wide)
    if share > 1:
        groups = [
            [(base * share + i) for i in range(share)] for base in range(ctx_count // share)
        ]
        both = lax.all_gather(
            jnp.stack([grad_k_rot, grad_v]), "c", axis=0, axis_index_groups=groups
        )
        both = jnp.sum(both, axis=0)
        grad_k_rot, grad_v = both[0], both[1]
    query_grad = (
        inverse_rotation(grad_q_rot, cosine_table, sine_table)
        .astype(low)
        .reshape(length, head_width)
    )
    key_grad = inverse_rotation(grad_k_rot[:, None], cosine_table, sine_table).astype(low)[:, 0]
    value_grad = grad_v.astype(low)
    if share > 1:
        key_grad = take(key_grad, (c % share) * kv_part, kv_part)
        value_grad = take(value_grad, (c % share) * kv_part, kv_part)
    packed = jnp.concatenate([query_grad, key_grad, value_grad], axis=1)
    packed_width = head_width + 2 * kv_part

    def unpack(rows_in):
        grid = rows_in.reshape(rows_in.shape[0], ctx_count, packed_width)
        flat = lambda piece: piece.reshape(rows_in.shape[0], -1)
        return (
            flat(grid[:, :, :head_width]),
            flat(grid[:, :, head_width : head_width + kv_part]),
            flat(grid[:, :, head_width + kv_part :]),
        )

    own_grads = unpack(lax.all_to_all(packed, "c", 0, 1, tiled=True))
    query_full = wires.over_fsdp(query_weight)
    key_full = wires.over_fsdp(key_matrix)
    value_full = wires.over_fsdp(value_matrix)
    grad_normed_one = (
        mm_t(own_grads[0], query_full)
        + mm_t(own_grads[1], key_full)
        + mm_t(own_grads[2], value_full)
    )
    scale_one = lax.rsqrt(jnp.mean(own_wide * own_wide, axis=-1, keepdims=True) + epsilon)
    grad_input_part, attn_gain_grad = rms_backward(
        own_wide, scale_one, attn_gain_f, grad_normed_one
    )
    input_grad = (grad_hidden + grad_input_part).astype(low).reshape(tokens.shape)

    packed_term = t_mm(normed_one, packed).reshape(ctx_count, 4, row_count, packed_width)
    packed_term = wires.sum_fsdp(packed_term, 1)
    packed_term = lax.all_to_all(packed_term, "c", 0, 0, tiled=True)
    query_out, key_out, value_out = unpack(
        packed_term.transpose(1, 0, 2).reshape(row_count, ctx_count * packed_width)
    )

    gain_parts = jnp.stack([attn_gain_grad, mlp_gain_grad]).reshape(2, 4 * ctx_count, row_count)
    gain_parts = lax.all_to_all(gain_parts.transpose(1, 0, 2), EVERY, 0, 0, tiled=True)
    gain_out = jnp.sum(gain_parts, axis=0)
    return (
        output,
        input_grad,
        gain_out[0],
        query_out,
        key_out,
        value_out,
        output_out,
        gain_out[1],
        gate_out,
        up_out,
        down_out,
    )


def solution(mesh):
    fsdp = ("x", "k")
    spread_all = ("c", "x", "k")
    ctx_count = mesh.shape["ctx"]
    grid = Mesh(mesh.devices.reshape(ctx_count, 2, 2), ("c", "x", "k"))
    row = P(fsdp, None)
    out_row = P(spread_all, None)
    act = P(fsdp, "c", None)
    return jax.shard_map(
        body,
        mesh=grid,
        in_specs=(act, act, P(), row, P(fsdp), row, row, row, row, P(fsdp), row, row, row),
        out_specs=(
            act,
            act,
            P(spread_all),
            out_row,
            out_row,
            out_row,
            out_row,
            P(spread_all),
            out_row,
            out_row,
            out_row,
        ),
        check_vma=False,
    )
```

time: 3960 us -> 957 us (0.24)
  waiting for transfers between devices: 3480 us -> 372 us
  starting transfers between devices: 1.19 us -> 215 us
  matrix products: 330 us -> 129 us
  other arithmetic: 13.2 us -> 119 us
  blocking collectives: 49.8 us -> 0 us
    reduce_scatter x9 -> x0, waiting for transfers between devices: 2750 us -> none  [the longest x1 713 us: body(): lax.psum_scatter(tail_term, ('ctx', 'fsdp'), scatter_dimension=0, tiled=T...]
    all_gather x9 -> x2, waiting for transfers between devices: 723 us -> 0.01 us  [ctx_gather(): return lax.all_gather(value, 'c', axis=0, tiled=False)]
    ppermute x0 -> x73, waiting for transfers between devices: none -> 306 us  [the longest x48 210 us: swap(): lax.ppermute(value, EVERY, [(i, i ^ bits) for i in range(self.total)])]
    dot_general x77 -> x31, matrix products: 330 us -> 118 us  [the longest x8 33.6 us: t_mm(): return jnp.einsum('ti,tj->ij', left, right, preferred_element_type=wide)]
    ppermute x0 -> x73, starting transfers between devices: none -> 158 us  [the longest x48 99.5 us: swap(): lax.ppermute(value, EVERY, [(i, i ^ bits) for i in range(self.total)])]
    all_to_all x0 -> x7, waiting for transfers between devices: none -> 66.4 us  [the longest x2 58.5 us: columns_out(): moved = lax.all_to_all(parts.astype(low), CHIPS, 0, 0, tiled=True)]
    another operation x6 -> x61, other arithmetic: 1.01 us -> 62.4 us  [the longest x11 28.3 us: over_fsdp(): return jnp.stack([even, odd], axis=1).reshape((-1,) + shard.shape[1:])]
    all_to_all x0 -> x7, starting transfers between devices: none -> 56.7 us  [the longest x1 20.6 us: body(): mixed_rows = lax.all_to_all(mixed, 'c', 0, 1, tiled=True)]
  transfers between devices with their start and end apart: 18 -> 82, of which waited for: 17 -> 34; matrix products, arithmetic and copies ran while one was open for 6% -> 27% of each run, Pallas kernels for 0% -> 0%
where the time goes in v1:
time: 957 us; the launch traced here: 944 us
  waiting for transfers between devices  372 us (39%)
  starting transfers between devices  215 us (22%)
  matrix products  129 us (13%)
  other arithmetic  119 us (12%)
  local copies, waits for them, and re-layouts  91.9 us (10%)
  between operations  16.9 us (2%)
    ppermute x48, waiting for transfers between devices, swap(): lax.ppermute(value, EVERY, [(i, i ^ bits) for i in range(self.total)])  210 us
    ppermute x48, starting transfers between devices, swap(): lax.ppermute(value, EVERY, [(i, i ^ bits) for i in range(self.total)])  99.5 us
    ppermute x25, waiting for transfers between devices, send(): return lax.ppermute(value, EVERY, pairs)  95.7 us
    ppermute x25, starting transfers between devices, send(): return lax.ppermute(value, EVERY, pairs)  58.8 us
    all_to_all x2, waiting for transfers between devices, columns_out(): moved = lax.all_to_all(parts.astype(low), CHIPS, 0, 0, tiled=True)  58.5 us
    dot_general x8, matrix products, t_mm(): return jnp.einsum('ti,tj->ij', left, right, preferred_element_type=wide)  33.6 us
    dot_general x10, matrix products, mm_t(): return jnp.einsum('ij,kj->ik', left, right, preferred_element_type=wide)  33.2 us
    another operation x11, other arithmetic, over_fsdp(): return jnp.stack([even, odd], axis=1).reshape((-1,) + shard.shape[1:])  28.3 us
  transfers between devices with their start and end apart: 82, of which 34 were waited for; matrix products, arithmetic and copies ran while one was open for 27% of the time, Pallas kernels for 0%

profile of v1, /device:TPU:14, one launch (start us, length us, event | category | flops | bytes accessed | tf_op | source)
XLA Modules:
  0.0 944.2 jit_solution(9852030335900377942)
XLA Ops:
  9.7 4.6 collective-permute-start.38
  42.7 9.3 collective-permute-done.15
  62.2 22.5 %collective-permute-done.49 = bf16[64,2048]{1,0:T(8,128)(2,1)S(1)} collective-permute-done((bf16[64,2048]{1,0:T(8,128)(2,1)S(1)}, bf16[64,2048]{1,0:T(8,128)(2,1)S(1)}, u32[]{:S(2)}, u32[]{:S(2)}) %collective-permute-start.49) | collective-permute-done | bytes 262176 | tf_op jit(solution)/shard_map/ppermute | solution.py:119
  87.8 15.9 %collective-permute-done.40 = bf16[64,2048]{1,0:T(8,128)(2,1)S(1)} collective-permute-done((bf16[64,2048]{1,0:T(8,128)(2,1)S(1)}, bf16[64,2048]{1,0:T(8,128)(2,1)S(1)}, u32[]{:S(2)}, u32[]{:S(2)}) %collective-permute-start.40) | collective-permute-done | bytes 262176 | tf_op jit(solution)/shard_map/ppermute | solution.py:119
  103.8 4.6 collective-permute-start.52
  126.2 15.9 %collective-permute-done.41 = bf16[4,64,2048]{2,1,0:T(8,128)(2,1)S(1)} collective-permute-done((bf16[4,64,2048]{2,1,0:T(8,128)(2,1)S(1)}, bf16[4,64,2048]{2,1,0:T(8,128)(2,1)S(1)}, u32[]{:S(2)}, u32[]{:S(2)}) %collective-permute-start.41) | collective-permute-done | bytes 1048608 | tf_op jit(solution)/shard_map/ppermute | solution.py:116
  150.8 36.4 %collective-permute-start.5 = (bf16[2,512,2048]{2,1,0:T(8,128)(2,1)}, bf16[2,512,2048]{2,1,0:T(8,128)(2,1)}, u32[]{:S(2)}, u32[]{:S(2)}) collective-permute-start(bf16[2,512,2048]{2,1,0:T(8,128)(2,1)} %pad_maximum_fusion.2), channel_id=1, source_target_pairs={{0,1},{1,0},{2,3},{3,2},{4,5},{5,4},{6,7},{7,6},{8,9},{9,8},{10,11... | collective-permute-start | bytes 12582920 | tf_op jit(solution)/shard_map/ppermute | solution.py:116
  187.3 3.7 dynamic-slice_select_fusion
  194.5 35.4 %collective-permute-start.61 = (bf16[2,512,2048]{2,1,0:T(8,128)(2,1)}, bf16[2,512,2048]{2,1,0:T(8,128)(2,1)}, u32[]{:S(2)}, u32[]{:S(2)}) collective-permute-start(bf16[2,512,2048]{2,1,0:T(8,128)(2,1)} %pad_maximum_fusion.7), channel_id=1, source_target_pairs={{0,1},{1,0},{2,3},{3,2},{4,5},{5,4},{6,7},{7,6},{8,9},{9,8},{10,11... | collective-permute-start | bytes 12582920 | tf_op jit(solution)/shard_map/ppermute | solution.py:116
  229.9 4.0 collective-permute-done.42
  245.0 11.0 %fusion.147 = (f32[4,1024]{1,0:T(4,128)S(1)}, f32[4,1024,1024]{1,2,0:T(8,128)}) fusion(pred[1024,1024]{0,1:T(8,128)(4,1)} %compare_and_fusion, bf16[1024,4,32]{0,2,1:T(8,128)(2,1)S(1)} %get-tuple-element.66, bf16[1024,4,32]{0,2,1:T(8,128)(2,1)S(1)} %get-tuple-element.65, bf16[1024,32]{0,1:T(8,128)(2,1)S(1)} %get-tuple-element.97, ...), kind=kOutput, calls=%fused_computation.358 | convolution fusion | flops 554959872 | bytes 18497536 | tf_op jit(solution)/shard_map/sub | solution.py:277
  256.0 7.4 fusion.28
  265.3 20.6 %all-to-all-start = ((bf16[8,128,256]{1,2,0:T(8,128)(2,1)}), bf16[8,128,256]{1,2,0:T(8,128)(2,1)S(1)}, u32[]{:S(2)}, u32[]{:S(2)}) async-start(bf16[8,128,256]{1,2,0:T(8,128)(2,1)} %copy.164), calls=%async_computation | async-start | bytes 1048576 | tf_op jit(solution)/shard_map/all_to_all | solution.py:286
  285.9 5.8 select_bitcast_fusion.3
  291.7 7.5 pad_maximum_fusion
  299.3 4.7 multiply_reduce_fusion.3
  310.4 4.0 pad_maximum_fusion.6
  332.4 4.2 collective-permute-done.25
  341.9 3.6 collective-permute-done.28
  345.8 18.4 %collective-permute-done.11 = bf16[4,64,2048]{2,1,0:T(8,128)(2,1)S(1)} collective-permute-done((bf16[4,64,2048]{2,1,0:T(8,128)(2,1)S(1)}, bf16[4,64,2048]{2,1,0:T(8,128)(2,1)S(1)}, u32[]{:S(2)}, u32[]{:S(2)}) %collective-permute-start.11) | collective-permute-done | bytes 1048608 | tf_op jit(solution)/shard_map/ppermute | solution.py:116
  368.0 5.2 select_bitcast_fusion.1
  373.1 7.6 pad_maximum_fusion.1
  380.7 8.5 copy.177
  395.9 6.6 copy.180
  402.5 12.4 %collective-permute-done.12 = bf16[2,4,64,2048]{3,2,1,0:T(8,128)(2,1)} collective-permute-done((bf16[2,4,64,2048]{3,2,1,0:T(8,128)(2,1)}, bf16[2,4,64,2048]{3,2,1,0:T(8,128)(2,1)}, u32[]{:S(2)}, u32[]{:S(2)}) %collective-permute-start.12) | collective-permute-done | bytes 2097184 | tf_op jit(solution)/shard_map/ppermute | solution.py:116
  422.9 13.5 %collective-permute-done.30 = bf16[2,4,64,2048]{3,2,1,0:T(8,128)(2,1)} collective-permute-done((bf16[2,4,64,2048]{3,2,1,0:T(8,128)(2,1)}, bf16[2,4,64,2048]{3,2,1,0:T(8,128)(2,1)}, u32[]{:S(2)}, u32[]{:S(2)}) %collective-permute-start.30) | collective-permute-done | bytes 2097184 | tf_op jit(solution)/shard_map/ppermute | solution.py:116
  438.4 3.6 fusion.153
  442.1 3.6 fusion.152
  458.3 4.3 multiply_convert_fusion.1
  477.3 4.4 fusion.159
  490.8 4.9 convolution_add_fusion.3
  509.1 4.7 fusion.160
  513.8 33.5 %collective-permute-done.19 = bf16[2,4,64,2048]{3,2,1,0:T(8,128)(2,1)S(1)} collective-permute-done((bf16[2,4,64,2048]{3,2,1,0:T(8,128)(2,1)S(1)}, bf16[2,4,64,2048]{3,2,1,0:T(8,128)(2,1)S(1)}, u32[]{:S(2)}, u32[]{:S(2)}) %collective-permute-start.19) | collective-permute-done | bytes 2097184 | tf_op jit(solution)/shard_map/ppermute | solution.py:116
  551.3 40.5 %collective-permute-done.43 = bf16[2,4,64,2048]{3,2,1,0:T(8,128)(2,1)S(1)} collective-permute-done((bf16[2,4,64,2048]{3,2,1,0:T(8,128)(2,1)}, bf16[2,4,64,2048]{3,2,1,0:T(8,128)(2,1)S(1)}, u32[]{:S(2)}, u32[]{:S(2)}) %collective-permute-start.43) | collective-permute-done | bytes 2097184 | tf_op jit(solution)/shard_map/ppermute | solution.py:116
  597.4 21.1 %collective-permute-done.20 = bf16[4,64,2048]{2,1,0:T(8,128)(2,1)S(1)} collective-permute-done((bf16[4,64,2048]{2,1,0:T(8,128)(2,1)S(1)}, bf16[4,64,2048]{2,1,0:T(8,128)(2,1)S(1)}, u32[]{:S(2)}, u32[]{:S(2)}) %collective-permute-start.20) | collective-permute-done | bytes 1048608 | tf_op jit(solution)/shard_map/ppermute | solution.py:116
  621.0 18.2 %collective-permute-done.44 = bf16[4,64,2048]{2,1,0:T(8,128)(2,1)S(1)} collective-permute-done((bf16[4,64,2048]{2,1,0:T(8,128)(2,1)S(1)}, bf16[4,64,2048]{2,1,0:T(8,128)(2,1)S(1)}, u32[]{:S(2)}, u32[]{:S(2)}) %collective-permute-start.44) | collective-permute-done | bytes 1048608 | tf_op jit(solution)/shard_map/ppermute | solution.py:116
  644.2 11.7 %collective-permute-done.33 = bf16[2,64,2048]{2,1,0:T(8,128)(2,1)S(1)} collective-permute-done((bf16[2,64,2048]{2,1,0:T(8,128)(2,1)S(1)}, bf16[2,64,2048]{2,1,0:T(8,128)(2,1)S(1)}, u32[]{:S(2)}, u32[]{:S(2)}) %collective-permute-start.33) | collective-permute-done | bytes 524320 | tf_op jit(solution)/shard_map/ppermute | solution.py:119
  655.9 5.0 collective-permute-start.22
  661.2 5.9 collective-permute-done.45
  667.1 5.0 collective-permute-start.34
  672.4 3.4 collective-permute-done.57
  675.8 5.0 collective-permute-start.46
  683.5 10.1 %collective-permute-done.46 = bf16[2,64,2048]{2,1,0:T(8,128)(2,1)S(1)} collective-permute-done((bf16[2,64,2048]{2,1,0:T(8,128)(2,1)S(1)}, bf16[2,64,2048]{2,1,0:T(8,128)(2,1)S(1)}, u32[]{:S(2)}, u32[]{:S(2)}) %collective-permute-start.46) | collective-permute-done | bytes 524320 | tf_op jit(solution)/shard_map/ppermute | solution.py:119
  693.8 8.0 collective-permute-done.58
  704.2 5.6 collective-permute-done.47
  715.4 6.4 convolution_convert_fusion
  722.7 5.7 all-to-all-start.1
  728.6 6.3 convolution_add_fusion.2
  745.6 6.9 all-to-all-start.6
  753.1 7.8 fusion.1
  760.9 7.9 fusion.3
  776.0 16.9 %all-to-all-done.6 = bf16[16,64,512]{2,1,0:T(8,128)(2,1)S(1)} async-done(((bf16[16,64,512]{2,1,0:T(8,128)(2,1)}), bf16[16,64,512]{2,1,0:T(8,128)(2,1)S(1)}, u32[]{:S(2)}, u32[]{:S(2)}) %all-to-all-start.6) | async-done | bytes 1048608 | tf_op jit(solution)/shard_map/all_to_all | solution.py:356
  792.9 6.2 all-to-all-start.5
  799.1 8.5 fusion.36
  808.7 41.6 %all-to-all-done.5 = bf16[16,64,512]{2,1,0:T(8,128)(2,1)S(1)} async-done(((bf16[16,64,512]{2,1,0:T(8,128)(2,1)}), bf16[16,64,512]{2,1,0:T(8,128)(2,1)S(1)}, u32[]{:S(2)}, u32[]{:S(2)}) %all-to-all-start.5) | async-done | bytes 1048608 | tf_op jit(solution)/shard_map/all_to_all | solution.py:356
  850.3 5.5 all-to-all-start.2
  855.8 4.0 bitcast_add_fusion.2
  863.2 4.9 fusion.54
  876.2 6.5 convolution_add_fusion.6
  890.0 3.4 fusion.10
  895.3 5.8 all-to-all-start.3
  901.2 7.4 collective-permute-done.67
  910.9 6.0 all-to-all-start.4
  925.2 7.9 all-to-all-done.4
  (529 shorter events, 269.5 us)
Async XLA Ops:
  7.2 229.1 %all-gather.4.cloned.1.call-start = ((), (), s32[]{:S(2)}) async-start(), calls=%async_computation.7 | async-start | bytes 4718592 | tf_op jit(solution)/shard_map/all_gather | solution.py:142
  9.2 25.2 %collective-permute-start.36 = (bf16[64,2048]{1,0:T(8,128)(2,1)}, bf16[64,2048]{1,0:T(8,128)(2,1)}, u32[]{:S(2)}, u32[]{:S(2)}) collective-permute-start(bf16[64,2048]{1,0:T(8,128)(2,1)} %get-tuple-element.87), channel_id=1, source_target_pairs={{0,8},{1,9},{2,10},{3,11},{4,12},{5,13},{6,14},{7,15},{8,0},{9,1},... | collective-permute-start | bytes 786440 | tf_op jit(solution)/shard_map/ppermute | solution.py:116
  9.7 26.7 %collective-permute-start.38 = (bf16[64,2048]{1,0:T(8,128)(2,1)}, bf16[64,2048]{1,0:T(8,128)(2,1)}, u32[]{:S(2)}, u32[]{:S(2)}) collective-permute-start(bf16[64,2048]{1,0:T(8,128)(2,1)} %get-tuple-element.87), channel_id=1, source_target_pairs={{8,16},{9,17},{10,18},{11,19},{12,20},{13,21},{14,22},{15,23},{16,... | collective-permute-start | bytes 786440 | tf_op jit(solution)/shard_map/ppermute | solution.py:119
  17.4 15.5 %collective-permute-start.2 = (bf16[512,384]{1,0:T(8,128)(2,1)S(1)}, bf16[512,384]{1,0:T(8,128)(2,1)}, u32[]{:S(2)}, u32[]{:S(2)}) collective-permute-start(bf16[512,384]{1,0:T(8,128)(2,1)S(1)} %pad_maximum_fusion.33), channel_id=1, source_target_pairs={{0,2},{1,3},{2,0},{3,1},{4,6},{5,7},{6,4},{7,5},{8,10},{9,11},{10,... | collective-permute-start | bytes 1179656 | tf_op jit(solution)/shard_map/ppermute | solution.py:116
  21.6 19.2 %collective-permute-start.13 = (bf16[512,512]{1,0:T(8,128)(2,1)}, bf16[512,512]{1,0:T(8,128)(2,1)S(1)}, u32[]{:S(2)}, u32[]{:S(2)}) collective-permute-start(bf16[512,512]{1,0:T(8,128)(2,1)} %constant_dynamic-slice_fusion.4), channel_id=1, source_target_pairs={{0,2},{1,3},{2,0},{3,1},{4,6},{5,7},{6,4},{7,5},{8,10},{9,11},{10,... | collective-permute-start | bytes 1572872 | tf_op jit(solution)/shard_map/ppermute | solution.py:116
  31.7 20.3 %collective-permute-start.15 = (bf16[512,512]{1,0:T(8,128)(2,1)}, bf16[512,512]{1,0:T(8,128)(2,1)S(1)}, u32[]{:S(2)}, u32[]{:S(2)}) collective-permute-start(bf16[512,512]{1,0:T(8,128)(2,1)} %constant_dynamic-slice_fusion.3), channel_id=1, source_target_pairs={{0,2},{1,3},{2,0},{3,1},{4,6},{5,7},{6,4},{7,5},{8,10},{9,11},{10,... | collective-permute-start | bytes 1572872 | tf_op jit(solution)/shard_map/ppermute | solution.py:116
  32.9 22.0 %collective-permute-start.48 = (bf16[64,2048]{1,0:T(8,128)(2,1)}, bf16[64,2048]{1,0:T(8,128)(2,1)S(1)}, u32[]{:S(2)}, u32[]{:S(2)}) collective-permute-start(bf16[64,2048]{1,0:T(8,128)(2,1)} %get-tuple-element.88), channel_id=1, source_target_pairs={{0,8},{1,9},{2,10},{3,11},{4,12},{5,13},{6,14},{7,15},{8,0},{9,1},... | collective-permute-start | bytes 786440 | tf_op jit(solution)/shard_map/ppermute | solution.py:116
  34.4 21.2 %collective-permute-start.50 = (bf16[64,2048]{1,0:T(8,128)(2,1)}, bf16[64,2048]{1,0:T(8,128)(2,1)S(1)}, u32[]{:S(2)}, u32[]{:S(2)}) collective-permute-start(bf16[64,2048]{1,0:T(8,128)(2,1)} %get-tuple-element.88), channel_id=1, source_target_pairs={{8,16},{9,17},{10,18},{11,19},{12,20},{13,21},{14,22},{15,23},{16,... | collective-permute-start | bytes 786440 | tf_op jit(solution)/shard_map/ppermute | solution.py:119
  36.5 49.1 %collective-permute-start.62 = (bf16[512,512]{1,0:T(8,128)(2,1)S(1)}, bf16[512,512]{1,0:T(8,128)(2,1)S(1)}, u32[]{:S(2)}, u32[]{:S(2)}) collective-permute-start(bf16[512,512]{1,0:T(8,128)(2,1)S(1)} %copy-done.62), channel_id=1, source_target_pairs={{0,2},{1,3},{2,0},{3,1},{4,6},{5,7},{6,4},{7,5},{8,10},{9,11},{10,... | collective-permute-start | bytes 1572872 | tf_op jit(solution)/shard_map/ppermute | solution.py:116
  40.8 17.9 %collective-permute-start.37 = (bf16[64,2048]{1,0:T(8,128)(2,1)}, bf16[64,2048]{1,0:T(8,128)(2,1)S(1)}, u32[]{:S(2)}, u32[]{:S(2)}) collective-permute-start(bf16[64,2048]{1,0:T(8,128)(2,1)} %collective-permute-done.36), channel_id=1, source_target_pairs={{8,16},{9,17},{10,18},{11,19},{12,20},{13,21},{14,22},{15,23},{16,... | collective-permute-start | bytes 786440 | tf_op jit(solution)/shard_map/ppermute | solution.py:119
  54.9 31.2 %collective-permute-start.64 = (bf16[512,512]{1,0:T(8,128)(2,1)S(1)}, bf16[512,512]{1,0:T(8,128)(2,1)S(1)}, u32[]{:S(2)}, u32[]{:S(2)}) collective-permute-start(bf16[512,512]{1,0:T(8,128)(2,1)S(1)} %copy-done.61), channel_id=1, source_target_pairs={{0,2},{1,3},{2,0},{3,1},{4,6},{5,7},{6,4},{7,5},{8,10},{9,11},{10,... | collective-permute-start | bytes 1572872 | tf_op jit(solution)/shard_map/ppermute | solution.py:116
  55.5 91.7 %collective-permute-start.4 = (bf16[512,2048]{1,0:T(8,128)(2,1)S(1)}, bf16[512,2048]{1,0:T(8,128)(2,1)S(1)}, u32[]{:S(2)}, u32[]{:S(2)}) collective-permute-start(bf16[512,2048]{1,0:T(8,128)(2,1)S(1)} %copy-done.46), channel_id=1, source_target_pairs={{0,2},{1,3},{2,0},{3,1},{4,6},{5,7},{6,4},{7,5},{8,10},{9,11},{10,... | collective-permute-start | bytes 6291464 | tf_op jit(solution)/shard_map/ppermute | solution.py:116
  58.7 26.0 %collective-permute-start.49 = (bf16[64,2048]{1,0:T(8,128)(2,1)S(1)}, bf16[64,2048]{1,0:T(8,128)(2,1)S(1)}, u32[]{:S(2)}, u32[]{:S(2)}) collective-permute-start(bf16[64,2048]{1,0:T(8,128)(2,1)S(1)} %collective-permute-done.48), channel_id=1, source_target_pairs={{8,16},{9,17},{10,18},{11,19},{12,20},{13,21},{14,22},{15,23},{16,... | collective-permute-start | bytes 786440 | tf_op jit(solution)/shard_map/ppermute | solution.py:119
  60.6 24.9 %collective-permute-start.51 = (bf16[64,2048]{1,0:T(8,128)(2,1)S(1)}, bf16[64,2048]{1,0:T(8,128)(2,1)S(1)}, u32[]{:S(2)}, u32[]{:S(2)}) collective-permute-start(bf16[64,2048]{1,0:T(8,128)(2,1)S(1)} %collective-permute-done.50), channel_id=1, source_target_pairs={{8,0},{9,1},{10,2},{11,3},{12,4},{13,5},{14,6},{15,7},{16,24},{17,... | collective-permute-start | bytes 786440 | tf_op jit(solution)/shard_map/ppermute | solution.py:119
  84.7 102.6 %collective-permute-start.17 = (bf16[512,2048]{1,0:T(8,128)(2,1)S(1)}, bf16[512,2048]{1,0:T(8,128)(2,1)S(1)}, u32[]{:S(2)}, u32[]{:S(2)}) collective-permute-start(bf16[512,2048]{1,0:T(8,128)(2,1)S(1)} %copy-done.42), channel_id=1, source_target_pairs={{0,2},{4,6},{9,11},{13,15},{18,16},{22,20},{27,25},{31,29}} | collective-permute-start | bytes 6291464 | tf_op jit(solution)/shard_map/ppermute | solution.py:119
  85.5 28.6 %collective-permute-start.3 = (bf16[2,512,384]{2,1,0:T(8,128)(2,1)S(1)}, bf16[2,512,384]{2,1,0:T(8,128)(2,1)S(1)}, u32[]{:S(2)}, u32[]{:S(2)}) collective-permute-start(bf16[2,512,384]{2,1,0:T(8,128)(2,1)S(1)} %pad_maximum_fusion.26), channel_id=1, source_target_pairs={{0,1},{1,0},{2,3},{3,2},{4,5},{5,4},{6,7},{7,6},{8,9},{9,8},{10,11... | collective-permute-start | bytes 2359304 | tf_op jit(solution)/shard_map/ppermute | solution.py:116
  85.6 30.5 %collective-permute-start.16 = (bf16[2,512,512]{2,1,0:T(8,128)(2,1)S(1)}, bf16[2,512,512]{2,1,0:T(8,128)(2,1)S(1)}, u32[]{:S(2)}, u32[]{:S(2)}) collective-permute-start(bf16[2,512,512]{2,1,0:T(8,128)(2,1)S(1)} %pad_maximum_fusion.19), channel_id=1, source_target_pairs={{0,1},{1,0},{2,3},{3,2},{4,5},{5,4},{6,7},{7,6},{8,9},{9,8},{10,11... | collective-permute-start | bytes 3145736 | tf_op jit(solution)/shard_map/ppermute | solution.py:116
  86.2 17.6 %collective-permute-start.40 = (bf16[64,2048]{1,0:T(8,128)(2,1)S(1)}, bf16[64,2048]{1,0:T(8,128)(2,1)S(1)}, u32[]{:S(2)}, u32[]{:S(2)}) collective-permute-start(bf16[64,2048]{1,0:T(8,128)(2,1)S(1)} %collective-permute-done.37), channel_id=1, source_target_pairs={{8,0},{9,1},{10,2},{11,3},{12,4},{13,5},{14,6},{15,7},{16,24},{17,... | collective-permute-start | bytes 786440 | tf_op jit(solution)/shard_map/ppermute | solution.py:119
  116.5 25.6 %collective-permute-start.41 = (bf16[4,64,2048]{2,1,0:T(8,128)(2,1)S(1)}, bf16[4,64,2048]{2,1,0:T(8,128)(2,1)S(1)}, u32[]{:S(2)}, u32[]{:S(2)}) collective-permute-start(bf16[4,64,2048]{2,1,0:T(8,128)(2,1)S(1)} %get-tuple-element.73), channel_id=1, source_target_pairs={{0,4},{1,5},{2,6},{3,7},{4,0},{5,1},{6,2},{7,3},{8,12},{9,13},{10,... | collective-permute-start | bytes 3145736 | tf_op jit(solution)/shard_map/ppermute | solution.py:116
  118.0 26.0 %collective-permute-start.53 = (bf16[4,64,2048]{2,1,0:T(8,128)(2,1)S(1)}, bf16[4,64,2048]{2,1,0:T(8,128)(2,1)S(1)}, u32[]{:S(2)}, u32[]{:S(2)}) collective-permute-start(bf16[4,64,2048]{2,1,0:T(8,128)(2,1)S(1)} %get-tuple-element.75), channel_id=1, source_target_pairs={{0,2},{1,3},{2,0},{3,1},{4,6},{5,7},{6,4},{7,5},{8,10},{9,11},{10,... | collective-permute-start | bytes 3145736 | tf_op jit(solution)/shard_map/ppermute | solution.py:116
  123.2 67.9 %collective-permute-start.60 = (bf16[512,2048]{1,0:T(8,128)(2,1)S(1)}, bf16[512,2048]{1,0:T(8,128)(2,1)S(1)}, u32[]{:S(2)}, u32[]{:S(2)}) collective-permute-start(bf16[512,2048]{1,0:T(8,128)(2,1)S(1)} %copy-done.39), channel_id=1, source_target_pairs={{0,2},{1,3},{2,0},{3,1},{4,6},{5,7},{6,4},{7,5},{8,10},{9,11},{10,... | collective-permute-start | bytes 6291464 | tf_op jit(solution)/shard_map/ppermute | solution.py:116
  142.4 91.5 %collective-permute-start.42 = (bf16[2,4,64,2048]{3,2,1,0:T(8,128)(2,1)S(1)}, bf16[2,4,64,2048]{3,2,1,0:T(8,128)(2,1)S(1)}, u32[]{:S(2)}, u32[]{:S(2)}) collective-permute-start(bf16[2,4,64,2048]{3,2,1,0:T(8,128)(2,1)S(1)} %get-tuple-element.50), channel_id=1, source_target_pairs={{0,2},{1,3},{2,0},{3,1},{4,6},{5,7},{6,4},{7,5},{8,10},{9,11},{10,... | collective-permute-start | bytes 6291464 | tf_op jit(solution)/shard_map/ppermute | solution.py:116
  146.3 164.0 %collective-permute-start.54 = (bf16[2,4,64,2048]{3,2,1,0:T(8,128)(2,1)}, bf16[2,4,64,2048]{3,2,1,0:T(8,128)(2,1)}, u32[]{:S(2)}, u32[]{:S(2)}) collective-permute-start(bf16[2,4,64,2048]{3,2,1,0:T(8,128)(2,1)} %get-tuple-element.52), channel_id=1, source_target_pairs={{0,4},{1,5},{2,6},{3,7},{4,0},{5,1},{6,2},{7,3},{8,12},{9,13},{10,... | collective-permute-start | bytes 6291464 | tf_op jit(solution)/shard_map/ppermute | solution.py:116
  150.8 135.0 %collective-permute-start.5 = (bf16[2,512,2048]{2,1,0:T(8,128)(2,1)}, bf16[2,512,2048]{2,1,0:T(8,128)(2,1)}, u32[]{:S(2)}, u32[]{:S(2)}) collective-permute-start(bf16[2,512,2048]{2,1,0:T(8,128)(2,1)} %pad_maximum_fusion.2), channel_id=1, source_target_pairs={{0,1},{1,0},{2,3},{3,2},{4,5},{5,4},{6,7},{7,6},{8,9},{9,8},{10,11... | collective-permute-start | bytes 12582920 | tf_op jit(solution)/shard_map/ppermute | solution.py:116
  191.0 123.4 %collective-permute-start.18 = (bf16[512,2048]{1,0:T(8,128)(2,1)}, bf16[512,2048]{1,0:T(8,128)(2,1)}, u32[]{:S(2)}, u32[]{:S(2)}) collective-permute-start(bf16[512,2048]{1,0:T(8,128)(2,1)} %dynamic-slice_select_fusion), channel_id=1, source_target_pairs={{0,1},{1,0},{2,3},{3,2},{4,5},{5,4},{6,7},{7,6},{8,9},{9,8},{10,11... | collective-permute-start | bytes 6291464 | tf_op jit(solution)/shard_map/ppermute | solution.py:116
  194.5 172.1 %collective-permute-start.61 = (bf16[2,512,2048]{2,1,0:T(8,128)(2,1)}, bf16[2,512,2048]{2,1,0:T(8,128)(2,1)}, u32[]{:S(2)}, u32[]{:S(2)}) collective-permute-start(bf16[2,512,2048]{2,1,0:T(8,128)(2,1)} %pad_maximum_fusion.7), channel_id=1, source_target_pairs={{0,1},{1,0},{2,3},{3,2},{4,5},{5,4},{6,7},{7,6},{8,9},{9,8},{10,11... | collective-permute-start | bytes 12582920 | tf_op jit(solution)/shard_map/ppermute | solution.py:116
  265.3 34.0 %all-to-all-start = ((bf16[8,128,256]{1,2,0:T(8,128)(2,1)}), bf16[8,128,256]{1,2,0:T(8,128)(2,1)S(1)}, u32[]{:S(2)}, u32[]{:S(2)}) async-start(bf16[8,128,256]{1,2,0:T(8,128)(2,1)} %copy.164), calls=%async_computation | async-start | bytes 1048576 | tf_op jit(solution)/shard_map/all_to_all | solution.py:286
  320.3 17.6 %collective-permute-start.9 = (bf16[64,2048]{1,0:T(8,128)(2,1)S(1)}, bf16[64,2048]{1,0:T(8,128)(2,1)S(1)}, u32[]{:S(2)}, u32[]{:S(2)}) collective-permute-start(bf16[64,2048]{1,0:T(8,128)(2,1)S(1)} %collective-permute-done.8), channel_id=1, source_target_pairs={{8,0},{9,1},{10,2},{11,3},{12,4},{13,5},{14,6},{15,7},{16,24},{17,... | collective-permute-start | bytes 786440 | tf_op jit(solution)/shard_map/ppermute | solution.py:119
  321.6 15.0 %collective-permute-start.25 = (bf16[64,2048]{1,0:T(8,128)(2,1)S(1)}, bf16[64,2048]{1,0:T(8,128)(2,1)S(1)}, u32[]{:S(2)}, u32[]{:S(2)}) collective-permute-start(bf16[64,2048]{1,0:T(8,128)(2,1)S(1)} %collective-permute-done.24), channel_id=1, source_target_pairs={{8,16},{9,17},{10,18},{11,19},{12,20},{13,21},{14,22},{15,23},{16,... | collective-permute-start | bytes 786440 | tf_op jit(solution)/shard_map/ppermute | solution.py:119
  327.5 14.4 %collective-permute-start.27 = (bf16[64,2048]{1,0:T(8,128)(2,1)S(1)}, bf16[64,2048]{1,0:T(8,128)(2,1)S(1)}, u32[]{:S(2)}, u32[]{:S(2)}) collective-permute-start(bf16[64,2048]{1,0:T(8,128)(2,1)S(1)} %collective-permute-done.26), channel_id=1, source_target_pairs={{8,0},{9,1},{10,2},{11,3},{12,4},{13,5},{14,6},{15,7},{16,24},{17,... | collective-permute-start | bytes 786440 | tf_op jit(solution)/shard_map/ppermute | solution.py:119
  341.3 22.9 %collective-permute-start.11 = (bf16[4,64,2048]{2,1,0:T(8,128)(2,1)S(1)}, bf16[4,64,2048]{2,1,0:T(8,128)(2,1)S(1)}, u32[]{:S(2)}, u32[]{:S(2)}) collective-permute-start(bf16[4,64,2048]{2,1,0:T(8,128)(2,1)S(1)} %get-tuple-element.77), channel_id=1, source_target_pairs={{0,4},{1,5},{2,6},{3,7},{4,0},{5,1},{6,2},{7,3},{8,12},{9,13},{10,... | collective-permute-start | bytes 3145736 | tf_op jit(solution)/shard_map/ppermute | solution.py:116
  345.7 43.5 %collective-permute-start.29 = (bf16[4,64,2048]{2,1,0:T(8,128)(2,1)S(1)}, bf16[4,64,2048]{2,1,0:T(8,128)(2,1)S(1)}, u32[]{:S(2)}, u32[]{:S(2)}) collective-permute-start(bf16[4,64,2048]{2,1,0:T(8,128)(2,1)S(1)} %get-tuple-element.79), channel_id=1, source_target_pairs={{0,2},{1,3},{2,0},{3,1},{4,6},{5,7},{6,4},{7,5},{8,10},{9,11},{10,... | collective-permute-start | bytes 3145736 | tf_op jit(solution)/shard_map/ppermute | solution.py:116
  366.6 48.2 %collective-permute-start.12 = (bf16[2,4,64,2048]{3,2,1,0:T(8,128)(2,1)}, bf16[2,4,64,2048]{3,2,1,0:T(8,128)(2,1)}, u32[]{:S(2)}, u32[]{:S(2)}) collective-permute-start(bf16[2,4,64,2048]{3,2,1,0:T(8,128)(2,1)} %get-tuple-element.54), channel_id=1, source_target_pairs={{0,2},{1,3},{2,0},{3,1},{4,6},{5,7},{6,4},{7,5},{8,10},{9,11},{10,... | collective-permute-start | bytes 6291464 | tf_op jit(solution)/shard_map/ppermute | solution.py:116
  391.6 44.8 %collective-permute-start.30 = (bf16[2,4,64,2048]{3,2,1,0:T(8,128)(2,1)}, bf16[2,4,64,2048]{3,2,1,0:T(8,128)(2,1)}, u32[]{:S(2)}, u32[]{:S(2)}) collective-permute-start(bf16[2,4,64,2048]{3,2,1,0:T(8,128)(2,1)} %get-tuple-element.60), channel_id=1, source_target_pairs={{0,4},{1,5},{2,6},{3,7},{4,0},{5,1},{6,2},{7,3},{8,12},{9,13},{10,... | collective-permute-start | bytes 6291464 | tf_op jit(solution)/shard_map/ppermute | solution.py:116
  498.8 239.3 %collective-permute-start.71 = (f32[16,64,512]{2,1,0:T(8,128)}, f32[16,64,512]{2,1,0:T(8,128)}, u32[]{:S(2)}, u32[]{:S(2)}) collective-permute-start(f32[16,64,512]{2,1,0:T(8,128)} %dynamic-slice_bitcast_fusion.1), channel_id=1, source_target_pairs={{0,1},{1,0},{2,3},{3,2},{4,5},{5,4},{6,7},{7,6},{8,9},{9,8},{10,11... | collective-permute-start | bytes 6291464 | tf_op jit(solution)/shard_map/ppermute | solution.py:116
  498.8 48.5 %collective-permute-start.19 = (bf16[2,4,64,2048]{3,2,1,0:T(8,128)(2,1)S(1)}, bf16[2,4,64,2048]{3,2,1,0:T(8,128)(2,1)S(1)}, u32[]{:S(2)}, u32[]{:S(2)}) collective-permute-start(bf16[2,4,64,2048]{3,2,1,0:T(8,128)(2,1)S(1)} %bitcast.514), channel_id=1, source_target_pairs={{0,2},{1,3},{2,0},{3,1},{4,6},{5,7},{6,4},{7,5},{8,10},{9,11},{10,... | collective-permute-start | bytes 6291464 | tf_op jit(solution)/shard_map/ppermute | solution.py:116
  499.2 49.7 %collective-permute-start.31 = (bf16[2,4,64,2048]{3,2,1,0:T(8,128)(2,1)}, bf16[2,4,64,2048]{3,2,1,0:T(8,128)(2,1)S(1)}, u32[]{:S(2)}, u32[]{:S(2)}) collective-permute-start(bf16[2,4,64,2048]{3,2,1,0:T(8,128)(2,1)} %bitcast.71), channel_id=1, source_target_pairs={{0,4},{1,5},{2,6},{3,7},{4,0},{5,1},{6,2},{7,3},{8,12},{9,13},{10,... | collective-permute-start | bytes 6291464 | tf_op jit(solution)/shard_map/ppermute | solution.py:116
  507.8 234.8 %collective-permute-start.70 = (f32[16,64,512]{2,1,0:T(8,128)}, f32[16,64,512]{2,1,0:T(8,128)}, u32[]{:S(2)}, u32[]{:S(2)}) collective-permute-start(f32[16,64,512]{2,1,0:T(8,128)} %dynamic-slice_bitcast_fusion.2), channel_id=1, source_target_pairs={{0,1},{1,0},{2,3},{3,2},{4,5},{5,4},{6,7},{7,6},{8,9},{9,8},{10,11... | collective-permute-start | bytes 6291464 | tf_op jit(solution)/shard_map/ppermute | solution.py:116
  507.8 84.0 %collective-permute-start.43 = (bf16[2,4,64,2048]{3,2,1,0:T(8,128)(2,1)}, bf16[2,4,64,2048]{3,2,1,0:T(8,128)(2,1)S(1)}, u32[]{:S(2)}, u32[]{:S(2)}) collective-permute-start(bf16[2,4,64,2048]{3,2,1,0:T(8,128)(2,1)} %bitcast.88), channel_id=1, source_target_pairs={{0,2},{1,3},{2,0},{3,1},{4,6},{5,7},{6,4},{7,5},{8,10},{9,11},{10,... | collective-permute-start | bytes 6291464 | tf_op jit(solution)/shard_map/ppermute | solution.py:116
  547.3 48.7 %collective-permute-start.55 = (bf16[2,4,64,2048]{3,2,1,0:T(8,128)(2,1)}, bf16[2,4,64,2048]{3,2,1,0:T(8,128)(2,1)S(1)}, u32[]{:S(2)}, u32[]{:S(2)}) collective-permute-start(bf16[2,4,64,2048]{3,2,1,0:T(8,128)(2,1)} %bitcast.103), channel_id=1, source_target_pairs={{0,4},{1,5},{2,6},{3,7},{4,0},{5,1},{6,2},{7,3},{8,12},{9,13},{10,... | collective-permute-start | bytes 6291464 | tf_op jit(solution)/shard_map/ppermute | solution.py:116
  548.9 69.6 %collective-permute-start.20 = (bf16[4,64,2048]{2,1,0:T(8,128)(2,1)S(1)}, bf16[4,64,2048]{2,1,0:T(8,128)(2,1)S(1)}, u32[]{:S(2)}, u32[]{:S(2)}) collective-permute-start(bf16[4,64,2048]{2,1,0:T(8,128)(2,1)S(1)} %fusion.49), channel_id=1, source_target_pairs={{0,4},{1,5},{2,6},{3,7},{4,0},{5,1},{6,2},{7,3},{8,12},{9,13},{10,... | collective-permute-start | bytes 3145736 | tf_op jit(solution)/shard_map/ppermute | solution.py:116
  591.8 27.6 %collective-permute-start.32 = (bf16[4,64,2048]{2,1,0:T(8,128)(2,1)S(1)}, bf16[4,64,2048]{2,1,0:T(8,128)(2,1)S(1)}, u32[]{:S(2)}, u32[]{:S(2)}) collective-permute-start(bf16[4,64,2048]{2,1,0:T(8,128)(2,1)S(1)} %fusion.50), channel_id=1, source_target_pairs={{0,2},{1,3},{2,0},{3,1},{4,6},{5,7},{6,4},{7,5},{8,10},{9,11},{10,... | collective-permute-start | bytes 3145736 | tf_op jit(solution)/shard_map/ppermute | solution.py:116
  596.0 43.2 %collective-permute-start.44 = (bf16[4,64,2048]{2,1,0:T(8,128)(2,1)S(1)}, bf16[4,64,2048]{2,1,0:T(8,128)(2,1)S(1)}, u32[]{:S(2)}, u32[]{:S(2)}) collective-permute-start(bf16[4,64,2048]{2,1,0:T(8,128)(2,1)S(1)} %fusion.51), channel_id=1, source_target_pairs={{0,4},{1,5},{2,6},{3,7},{4,0},{5,1},{6,2},{7,3},{8,12},{9,13},{10,... | collective-permute-start | bytes 3145736 | tf_op jit(solution)/shard_map/ppermute | solution.py:116
  618.5 22.4 %collective-permute-start.56 = (bf16[4,64,2048]{2,1,0:T(8,128)(2,1)S(1)}, bf16[4,64,2048]{2,1,0:T(8,128)(2,1)S(1)}, u32[]{:S(2)}, u32[]{:S(2)}) collective-permute-start(bf16[4,64,2048]{2,1,0:T(8,128)(2,1)S(1)} %fusion.52), channel_id=1, source_target_pairs={{0,2},{1,3},{2,0},{3,1},{4,6},{5,7},{6,4},{7,5},{8,10},{9,11},{10,... | collective-permute-start | bytes 3145736 | tf_op jit(solution)/shard_map/ppermute | solution.py:116
  619.4 23.2 %collective-permute-start.21 = (bf16[2,64,2048]{2,1,0:T(8,128)(2,1)S(1)}, bf16[2,64,2048]{2,1,0:T(8,128)(2,1)S(1)}, u32[]{:S(2)}, u32[]{:S(2)}) collective-permute-start(bf16[2,64,2048]{2,1,0:T(8,128)(2,1)S(1)} %stack.441), channel_id=1, source_target_pairs={{0,8},{1,9},{2,10},{3,11},{4,12},{5,13},{6,14},{7,15},{24,16},{25,... | collective-permute-start | bytes 1572872 | tf_op jit(solution)/shard_map/ppermute | solution.py:119
  639.2 16.7 %collective-permute-start.33 = (bf16[2,64,2048]{2,1,0:T(8,128)(2,1)S(1)}, bf16[2,64,2048]{2,1,0:T(8,128)(2,1)S(1)}, u32[]{:S(2)}, u32[]{:S(2)}) collective-permute-start(bf16[2,64,2048]{2,1,0:T(8,128)(2,1)S(1)} %stack.440), channel_id=1, source_target_pairs={{0,8},{1,9},{2,10},{3,11},{4,12},{5,13},{6,14},{7,15},{24,16},{25,... | collective-permute-start | bytes 1572872 | tf_op jit(solution)/shard_map/ppermute | solution.py:119
  640.9 26.2 %collective-permute-start.45 = (bf16[2,64,2048]{2,1,0:T(8,128)(2,1)S(1)}, bf16[2,64,2048]{2,1,0:T(8,128)(2,1)S(1)}, u32[]{:S(2)}, u32[]{:S(2)}) collective-permute-start(bf16[2,64,2048]{2,1,0:T(8,128)(2,1)S(1)} %stack.439), channel_id=1, source_target_pairs={{0,8},{1,9},{2,10},{3,11},{4,12},{5,13},{6,14},{7,15},{24,16},{25,... | collective-permute-start | bytes 1572872 | tf_op jit(solution)/shard_map/ppermute | solution.py:119
  642.5 33.3 %collective-permute-start.57 = (bf16[2,64,2048]{2,1,0:T(8,128)(2,1)S(1)}, bf16[2,64,2048]{2,1,0:T(8,128)(2,1)S(1)}, u32[]{:S(2)}, u32[]{:S(2)}) collective-permute-start(bf16[2,64,2048]{2,1,0:T(8,128)(2,1)S(1)} %stack.438), channel_id=1, source_target_pairs={{0,8},{1,9},{2,10},{3,11},{4,12},{5,13},{6,14},{7,15},{24,16},{25,... | collective-permute-start | bytes 1572872 | tf_op jit(solution)/shard_map/ppermute | solution.py:119
  655.9 25.3 %collective-permute-start.22 = (bf16[2,64,2048]{2,1,0:T(8,128)(2,1)S(1)}, bf16[2,64,2048]{2,1,0:T(8,128)(2,1)S(1)}, u32[]{:S(2)}, u32[]{:S(2)}) collective-permute-start(bf16[2,64,2048]{2,1,0:T(8,128)(2,1)S(1)} %pad_maximum_fusion.29), channel_id=1, source_target_pairs={{8,16},{9,17},{10,18},{11,19},{12,20},{13,21},{14,22},{15,23},{16,... | collective-permute-start | bytes 1572872 | tf_op jit(solution)/shard_map/ppermute | solution.py:119
  667.1 16.2 %collective-permute-start.34 = (bf16[2,64,2048]{2,1,0:T(8,128)(2,1)S(1)}, bf16[2,64,2048]{2,1,0:T(8,128)(2,1)S(1)}, u32[]{:S(2)}, u32[]{:S(2)}) collective-permute-start(bf16[2,64,2048]{2,1,0:T(8,128)(2,1)S(1)} %pad_maximum_fusion.30), channel_id=1, source_target_pairs={{8,16},{9,17},{10,18},{11,19},{12,20},{13,21},{14,22},{15,23},{16,... | collective-permute-start | bytes 1572872 | tf_op jit(solution)/shard_map/ppermute | solution.py:119
  675.8 17.8 %collective-permute-start.46 = (bf16[2,64,2048]{2,1,0:T(8,128)(2,1)S(1)}, bf16[2,64,2048]{2,1,0:T(8,128)(2,1)S(1)}, u32[]{:S(2)}, u32[]{:S(2)}) collective-permute-start(bf16[2,64,2048]{2,1,0:T(8,128)(2,1)S(1)} %pad_maximum_fusion.31), channel_id=1, source_target_pairs={{8,16},{9,17},{10,18},{11,19},{12,20},{13,21},{14,22},{15,23},{16,... | collective-permute-start | bytes 1572872 | tf_op jit(solution)/shard_map/ppermute | solution.py:119
  681.2 20.6 %collective-permute-start.58 = (bf16[2,64,2048]{2,1,0:T(8,128)(2,1)S(1)}, bf16[2,64,2048]{2,1,0:T(8,128)(2,1)S(1)}, u32[]{:S(2)}, u32[]{:S(2)}) collective-permute-start(bf16[2,64,2048]{2,1,0:T(8,128)(2,1)S(1)} %pad_maximum_fusion.32), channel_id=1, source_target_pairs={{8,16},{9,17},{10,18},{11,19},{12,20},{13,21},{14,22},{15,23},{16,... | collective-permute-start | bytes 1572872 | tf_op jit(solution)/shard_map/ppermute | solution.py:119
  683.3 18.6 %collective-permute-start.23 = (bf16[64,2048]{1,0:T(8,128)(2,1)S(1)}, bf16[64,2048]{1,0:T(8,128)(2,1)S(1)}, u32[]{:S(2)}, u32[]{:S(2)}) collective-permute-start(bf16[64,2048]{1,0:T(8,128)(2,1)S(1)} %fusion.83), channel_id=1, source_target_pairs={{0,8},{1,9},{2,10},{3,11},{4,12},{5,13},{6,14},{7,15},{8,0},{9,1},... | collective-permute-start | bytes 786440 | tf_op jit(solution)/shard_map/ppermute | solution.py:116
  693.6 19.4 %collective-permute-start.35 = (bf16[64,2048]{1,0:T(8,128)(2,1)S(1)}, bf16[64,2048]{1,0:T(8,128)(2,1)S(1)}, u32[]{:S(2)}, u32[]{:S(2)}) collective-permute-start(bf16[64,2048]{1,0:T(8,128)(2,1)S(1)} %fusion.84), channel_id=1, source_target_pairs={{0,8},{1,9},{2,10},{3,11},{4,12},{5,13},{6,14},{7,15},{8,0},{9,1},... | collective-permute-start | bytes 786440 | tf_op jit(solution)/shard_map/ppermute | solution.py:116
  722.7 22.8 %all-to-all-start.1 = ((bf16[128,8,256]{2,0,1:T(8,128)(2,1)}), bf16[128,8,256]{2,0,1:T(8,128)(2,1)S(1)}, u32[]{:S(2)}, u32[]{:S(2)}) async-start(bf16[128,8,256]{2,0,1:T(8,128)(2,1)} %bitcast.463), calls=%async_computation.1 | async-start | bytes 1048576 | tf_op jit(solution)/shard_map/all_to_all | solution.py:366
  728.4 161.6 %all-gather.6.cloned.1.call-start = ((), (), s32[]{:S(2)}) async-start(), calls=%async_computation.8 | async-start | bytes 4718592 | tf_op jit(solution)/shard_map/all_gather | solution.py:142
  738.1 117.8 %collective-permute-start.72 = (f32[256,2048]{1,0:T(8,128)}, f32[256,2048]{1,0:T(8,128)}, u32[]{:S(2)}, u32[]{:S(2)}) collective-permute-start(f32[256,2048]{1,0:T(8,128)} %dynamic-slice_bitcast_fusion), channel_id=1, source_target_pairs={{0,1},{1,0},{2,3},{3,2},{4,5},{5,4},{6,7},{7,6},{8,9},{9,8},{10,11... | collective-permute-start | bytes 6291464 | tf_op jit(solution)/shard_map/ppermute | solution.py:116
  745.6 47.4 %all-to-all-start.6 = ((bf16[16,64,512]{2,1,0:T(8,128)(2,1)}), bf16[16,64,512]{2,1,0:T(8,128)(2,1)S(1)}, u32[]{:S(2)}, u32[]{:S(2)}) async-start(bf16[16,64,512]{2,1,0:T(8,128)(2,1)} %fusion.20), calls=%async_computation.6 | async-start | bytes 2097152 | tf_op jit(solution)/shard_map/all_to_all | solution.py:356
  792.9 57.4 %all-to-all-start.5 = ((bf16[16,64,512]{2,1,0:T(8,128)(2,1)}), bf16[16,64,512]{2,1,0:T(8,128)(2,1)S(1)}, u32[]{:S(2)}, u32[]{:S(2)}) async-start(bf16[16,64,512]{2,1,0:T(8,128)(2,1)} %fusion.21), calls=%async_computation.5 | async-start | bytes 2097152 | tf_op jit(solution)/shard_map/all_to_all | solution.py:356
  850.3 24.3 %all-to-all-start.2 = ((bf16[8,128,384]{1,2,0:T(8,128)(2,1)}), bf16[8,128,384]{1,2,0:T(8,128)(2,1)S(1)}, u32[]{:S(2)}, u32[]{:S(2)}) async-start(bf16[8,128,384]{1,2,0:T(8,128)(2,1)} %pad_maximum_fusion.27), calls=%async_computation.2 | async-start | bytes 1572864 | tf_op jit(solution)/shard_map/all_to_all | solution.py:413
  888.5 20.0 %collective-permute-start.67 = (f32[8,64,384]{2,1,0:T(8,128)}, f32[8,64,384]{2,1,0:T(8,128)}, u32[]{:S(2)}, u32[]{:S(2)}) collective-permute-start(f32[8,64,384]{2,1,0:T(8,128)} %dynamic-slice_bitcast_fusion.4), channel_id=1, source_target_pairs={{0,2},{1,3},{2,0},{3,1},{4,6},{5,7},{6,4},{7,5},{8,10},{9,11},{10,... | collective-permute-start | bytes 2359304 | tf_op jit(solution)/shard_map/ppermute | solution.py:116
  894.6 26.4 %collective-permute-start.68 = (f32[2,64,2048]{2,1,0:T(8,128)}, f32[2,64,2048]{2,1,0:T(8,128)}, u32[]{:S(2)}, u32[]{:S(2)}) collective-permute-start(f32[2,64,2048]{2,1,0:T(8,128)} %dynamic-slice_bitcast_fusion.3), channel_id=1, source_target_pairs={{0,1},{1,0},{2,3},{3,2},{4,5},{5,4},{6,7},{7,6},{8,9},{9,8},{10,11... | collective-permute-start | bytes 3145736 | tf_op jit(solution)/shard_map/ppermute | solution.py:116
  895.3 15.6 %all-to-all-start.3 = ((f32[32,1,128]{2,1,0:T(1,128)}), f32[32,1,128]{2,1,0:T(1,128)S(1)}, u32[]{:S(2)}, u32[]{:S(2)}) async-start(f32[32,1,128]{2,1,0:T(1,128)} %reshape.564), calls=%async_computation.3 | async-start | bytes 32768 | tf_op jit(solution)/shard_map/all_to_all | solution.py:436
  910.9 22.2 %all-to-all-start.4 = ((f32[8,64,384]{2,1,0:T(8,128)}), f32[8,64,384]{2,1,0:T(8,128)S(1)}, u32[]{:S(2)}, u32[]{:S(2)}) async-start(f32[8,64,384]{2,1,0:T(8,128)} %bitcast_add_fusion.4), calls=%async_computation.4 | async-start | bytes 1572864 | tf_op jit(solution)/shard_map/all_to_all | solution.py:430
  (113 other events, 1842.4 us)
Sparse Core Ops, SparseCore 0:
  19.8 82.0 all-gather.3
  745.7 108.3 all-gather.5
